TPU v7x, 32 devices: a whole 2x2x4 slice. The times are simulated.
32 devices in a mesh: bx: 8 (over z, x), bz: 4 (over y, core).
Axes of the slice: x: 2, y: 2, z: 4, core: 2. Of those that a mesh axis runs over, the one named last changes fastest.
Arguments:
- fields: bfloat16 [4, 32, 1024, 2048], P(None, 'bz', None, 'bx'), may hold values from -6 to 6
- breakpoints: int32 [8], replicated, may hold values from 0 to 255, as said below
- tf_color: float32 [8, 3], replicated, may hold values from 0.05 to 1
- tf_opacity: float32 [8], replicated, may hold values from 0.002 to 0.02
- depth_order: int32 [8, 4], replicated, may hold values from 0 to 3, each once within a row
- live_rows: int32 [8, 4, 2], P('bx', 'bz'), may hold values from 0 to 1024, as said below
Outputs:
- image: float32 [4, 1024, 2048], P(None, ('bx', 'bz'))
Inputs may be any that keep to these rules, and one draw needn't show every extreme that they name: `breakpoints`: strictly increasing, first 0 and last 255. `live_rows`: for every brick the first row is below 512 and the end row above it; some brick starts at row 0 and some ends at row 1024.
All inputs are finite; a program needn't handle non-finite values.
Results may differ from a plain program's by a relative error of at most 0.0003.
Values may be sent and summed in bfloat16 or wider, within the bound.
A program may use at most 128 MiB of HBM per device.

v0:
```python
import jax
import jax.numpy as jnp
from jax import lax
from jax.sharding import PartitionSpec as P

NBP = 8


def from_behind(block, axis, distance):
    devices = range(lax.axis_size(axis))
    route = [(i - distance, i) for i in devices if i - distance in devices]
    return lax.ppermute(block, axis, route)


def classify(raw, breakpoints, tf_color, tf_opacity):
    level = 255.0 * jax.nn.sigmoid(raw[0])
    swirl = raw[1] * raw[1] + raw[2] * raw[2] + raw[3] * raw[3]
    marks = breakpoints.astype(jnp.float32)
    ramps = []
    for j in range(1, NBP):
        ramps.append(jnp.clip((level - marks[j - 1]) / (marks[j] - marks[j - 1]), 0.0, 1.0))

    def lookup(values):
        total = values[0] + jnp.zeros_like(level)
        for j in range(1, NBP):
            total = total + (values[j] - values[j - 1]) * ramps[j - 1]
        return total

    alpha = 1.0 - jnp.exp(-lookup(tf_opacity) * (0.25 + swirl))
    return jnp.stack(
        [
            alpha * lookup(tf_color[:, 0]),
            alpha * lookup(tf_color[:, 1]),
            alpha * lookup(tf_color[:, 2]),
            alpha,
        ]
    )


def composite(gathered, order_rows):
    depth_count = gathered.shape[2]
    slots = jnp.arange(depth_count, dtype=jnp.int32)
    result = jnp.zeros((4, gathered.shape[1], gathered.shape[3], gathered.shape[4]), jnp.float32)
    for k in range(depth_count):
        pick = (order_rows[:, k][:, None] == slots[None, :]).astype(jnp.float32)
        chosen = jnp.sum(gathered * pick[None, :, :, None, None], axis=2)
        result = result + (1.0 - result[3:4]) * chosen
    return result


def per_device(fields, breakpoints, tf_color, tf_opacity, depth_order, live_rows):
    width = fields.shape[3]
    slices = fields.shape[1]
    height = fields.shape[2]
    count_x = lax.axis_size("bx")
    count_z = lax.axis_size("bz")
    reach = 3 * (slices * count_z - 1) // 8 + 1
    rim = from_behind(fields[:, :, :, width - reach :], "bx", 1)
    edge = (lax.axis_index("bx") > 0).astype(jnp.float32)
    column_keep = jnp.concatenate(
        [jnp.zeros((reach,), jnp.float32) + edge, jnp.ones((width,), jnp.float32)]
    )
    zbase = lax.axis_index("bz") * slices

    def advance(k, acc):
        raw = jnp.concatenate(
            [
                lax.dynamic_index_in_dim(rim, k, 1, keepdims=False),
                lax.dynamic_index_in_dim(fields, k, 1, keepdims=False),
            ],
            axis=2,
        ).astype(jnp.float32)
        sample = classify(raw, breakpoints, tf_color, tf_opacity) * column_keep[None, None, :]
        zglobal = zbase + k
        whole = 3 * zglobal // 8
        frac = (3 * zglobal % 8).astype(jnp.float32) / 8.0
        near = lax.dynamic_slice_in_dim(sample, reach - whole, width, 2)
        far = lax.dynamic_slice_in_dim(sample, reach - whole - 1, width, 2)
        return acc + (1.0 - acc[3:4]) * ((1.0 - frac) * near + frac * far)

    partial_value = lax.fori_loop(0, slices, advance, jnp.zeros((4, height, width), jnp.float32))
    rows = jnp.arange(height, dtype=jnp.int32)
    keep = ((rows >= live_rows[0, 0, 0]) & (rows < live_rows[0, 0, 1])).astype(jnp.float32)
    partial_value = partial_value * keep[None, :, None]
    owned = height // (count_x * count_z)
    pieces = partial_value.reshape(4, count_x, count_z, owned, width)
    arrived = lax.all_to_all(pieces, "bz", split_axis=2, concat_axis=2, tiled=True)
    own_order = lax.dynamic_slice_in_dim(depth_order, lax.axis_index("bx"), 1, 0)
    merged = composite(arrived, own_order)
    moved = lax.all_to_all(merged, "bx", split_axis=1, concat_axis=3, tiled=True)
    image = moved.reshape(4, owned, count_x * width)
    return image


def solution(mesh):
    return jax.shard_map(
        per_device,
        mesh=mesh,
        in_specs=(P(None, "bz", None, "bx"), P(), P(), P(), P(), P("bx", "bz", None)),
        out_specs=P(None, ("bx", "bz"), None),
        check_vma=False,
    )
```

profile of v0, /device:TPU:0, one launch (start us, length us, event | category | flops | bytes accessed | tf_op | source)
XLA Modules:
  0.0 495.0 jit_solution(11255290638026318071)
XLA Ops:
  0.0 9.0 %slice.651 = bf16[4,8,1024,12]{3,2,1,0:T(8,128)(2,1)} slice(bf16[4,8,1024,256]{3,2,1,0:T(8,128)(2,1)} %param.8), slice={[0:4], [0:8], [0:1024], [244:256]} | slice | bytes 1572864 | tf_op jit(solution)/shard_map/slice | solution.py:58
  9.0 7.3 %copy.33 = bf16[4,8,1024,12]{2,1,3,0:T(8,128)(2,1)S(1)} copy(bf16[4,8,1024,12]{3,2,1,0:T(8,128)(2,1)} %slice.651) | data formatting | bytes 1572864
  69.9 330.5 %while.19 = (s32[]{:T(128)}, f32[4,1024,256]{2,1,0:T(8,128)}, s32[]{:T(128)}, f32[8]{0:T(128)S(1)}, f32[]{:T(128)}, /*index=5*/bf16[4,8,1024,12]{2,1,3,0:T(8,128...) while((s32[]{:T(128)}, f32[4,1024,256]{2,1,0:T(8,128)}, ...), condition=%wide.region_1.2_spmd.clone, body=%wide.region_0.1_spmd.clone.sunk | while | flops 55627776 | bytes 85297456 | solution.py:81
  75.4 8.4 %add_multiply_fusion.6 = (f32[1,1024,268]{2,1,0:T(8,128)S(1)}, f32[1,1024,268]{2,1,0:T(8,128)S(1)}) fusion(f32[]{:T(128)} %get-tuple-element.1674, f32[]{:T(128)} %get-tuple-element.1673, f32[]{:T(128)} %get-tuple-element.1672, f32[]{:T(128)} %get-tuple-element.1671, f32[]{:T(128)} %get-tuple-element.1670, f32[]{:T(128)} %get-tuple-element.1669, ...), kind=kLoop, calls=%fused_computation.21.clone.1 | loop fusion | flops 17289216 | bytes 6586488 | tf_op jit(solution)/shard_map/while/body/eval_jaxpr/mul | solution.py:32
  91.0 7.3 %add_multiply_fusion.7 = f32[1,1024,268]{2,1,0:T(8,128)S(1)} fusion(f32[1,1024,268]{2,1,0:T(8,128)S(1)} %get-tuple-element.1530, f32[]{:T(128)} %get-tuple-element.1688, f32[]{:T(128)} %get-tuple-element.1687, f32[]{:T(128)} %get-tuple-element.1686, f32[]{:T(128)} %get-tuple-element.1685, f32[]{:T(128)} %get-tuple-element.1684, ...), kind=kLoop, calls=%fused_computation.19.clone.1 | loop fusion | flops 10977280 | bytes 3293272 | tf_op jit(solution)/shard_map/while/body/eval_jaxpr/mul | solution.py:34
  113.6 8.4 %add_multiply_fusion.6 = (f32[1,1024,268]{2,1,0:T(8,128)S(1)}, f32[1,1024,268]{2,1,0:T(8,128)S(1)}) fusion(f32[]{:T(128)} %get-tuple-element.1674, f32[]{:T(128)} %get-tuple-element.1673, f32[]{:T(128)} %get-tuple-element.1672, f32[]{:T(128)} %get-tuple-element.1671, f32[]{:T(128)} %get-tuple-element.1670, f32[]{:T(128)} %get-tuple-element.1669, ...), kind=kLoop, calls=%fused_computation.21.clone.1 | loop fusion | flops 17289216 | bytes 6586488 | tf_op jit(solution)/shard_map/while/body/eval_jaxpr/mul | solution.py:32
  129.2 7.3 %add_multiply_fusion.7 = f32[1,1024,268]{2,1,0:T(8,128)S(1)} fusion(f32[1,1024,268]{2,1,0:T(8,128)S(1)} %get-tuple-element.1530, f32[]{:T(128)} %get-tuple-element.1688, f32[]{:T(128)} %get-tuple-element.1687, f32[]{:T(128)} %get-tuple-element.1686, f32[]{:T(128)} %get-tuple-element.1685, f32[]{:T(128)} %get-tuple-element.1684, ...), kind=kLoop, calls=%fused_computation.19.clone.1 | loop fusion | flops 10977280 | bytes 3293272 | tf_op jit(solution)/shard_map/while/body/eval_jaxpr/mul | solution.py:34
  155.4 8.4 %add_multiply_fusion.6 = (f32[1,1024,268]{2,1,0:T(8,128)S(1)}, f32[1,1024,268]{2,1,0:T(8,128)S(1)}) fusion(f32[]{:T(128)} %get-tuple-element.1674, f32[]{:T(128)} %get-tuple-element.1673, f32[]{:T(128)} %get-tuple-element.1672, f32[]{:T(128)} %get-tuple-element.1671, f32[]{:T(128)} %get-tuple-element.1670, f32[]{:T(128)} %get-tuple-element.1669, ...), kind=kLoop, calls=%fused_computation.21.clone.1 | loop fusion | flops 17289216 | bytes 6586488 | tf_op jit(solution)/shard_map/while/body/eval_jaxpr/mul | solution.py:32
  163.8 7.1 %add_multiply_fusion.8 = f32[1,1024,268]{2,1,0:T(8,128)S(1)} fusion(f32[1,1024,268]{2,1,0:T(8,128)S(1)} %get-tuple-element.1530, f32[]{:T(128)} %get-tuple-element.1681, f32[]{:T(128)} %get-tuple-element.1680, f32[]{:T(128)} %get-tuple-element.1679, f32[]{:T(128)} %get-tuple-element.1678, f32[]{:T(128)} %get-tuple-element.1677, ...), kind=kLoop, calls=%fused_computation.20.clone.1 | loop fusion | flops 10977280 | bytes 3293272 | tf_op jit(solution)/shard_map/while/body/eval_jaxpr/mul | solution.py:33
  170.9 7.3 %add_multiply_fusion.7 = f32[1,1024,268]{2,1,0:T(8,128)S(1)} fusion(f32[1,1024,268]{2,1,0:T(8,128)S(1)} %get-tuple-element.1530, f32[]{:T(128)} %get-tuple-element.1688, f32[]{:T(128)} %get-tuple-element.1687, f32[]{:T(128)} %get-tuple-element.1686, f32[]{:T(128)} %get-tuple-element.1685, f32[]{:T(128)} %get-tuple-element.1684, ...), kind=kLoop, calls=%fused_computation.19.clone.1 | loop fusion | flops 10977280 | bytes 3293272 | tf_op jit(solution)/shard_map/while/body/eval_jaxpr/mul | solution.py:34
  197.1 8.4 %add_multiply_fusion.6 = (f32[1,1024,268]{2,1,0:T(8,128)S(1)}, f32[1,1024,268]{2,1,0:T(8,128)S(1)}) fusion(f32[]{:T(128)} %get-tuple-element.1674, f32[]{:T(128)} %get-tuple-element.1673, f32[]{:T(128)} %get-tuple-element.1672, f32[]{:T(128)} %get-tuple-element.1671, f32[]{:T(128)} %get-tuple-element.1670, f32[]{:T(128)} %get-tuple-element.1669, ...), kind=kLoop, calls=%fused_computation.21.clone.1 | loop fusion | flops 17289216 | bytes 6586488 | tf_op jit(solution)/shard_map/while/body/eval_jaxpr/mul | solution.py:32
  212.7 7.3 %add_multiply_fusion.7 = f32[1,1024,268]{2,1,0:T(8,128)S(1)} fusion(f32[1,1024,268]{2,1,0:T(8,128)S(1)} %get-tuple-element.1530, f32[]{:T(128)} %get-tuple-element.1688, f32[]{:T(128)} %get-tuple-element.1687, f32[]{:T(128)} %get-tuple-element.1686, f32[]{:T(128)} %get-tuple-element.1685, f32[]{:T(128)} %get-tuple-element.1684, ...), kind=kLoop, calls=%fused_computation.19.clone.1 | loop fusion | flops 10977280 | bytes 3293272 | tf_op jit(solution)/shard_map/while/body/eval_jaxpr/mul | solution.py:34
  238.9 8.4 %add_multiply_fusion.6 = (f32[1,1024,268]{2,1,0:T(8,128)S(1)}, f32[1,1024,268]{2,1,0:T(8,128)S(1)}) fusion(f32[]{:T(128)} %get-tuple-element.1674, f32[]{:T(128)} %get-tuple-element.1673, f32[]{:T(128)} %get-tuple-element.1672, f32[]{:T(128)} %get-tuple-element.1671, f32[]{:T(128)} %get-tuple-element.1670, f32[]{:T(128)} %get-tuple-element.1669, ...), kind=kLoop, calls=%fused_computation.21.clone.1 | loop fusion | flops 17289216 | bytes 6586488 | tf_op jit(solution)/shard_map/while/body/eval_jaxpr/mul | solution.py:32
  247.3 7.1 %add_multiply_fusion.8 = f32[1,1024,268]{2,1,0:T(8,128)S(1)} fusion(f32[1,1024,268]{2,1,0:T(8,128)S(1)} %get-tuple-element.1530, f32[]{:T(128)} %get-tuple-element.1681, f32[]{:T(128)} %get-tuple-element.1680, f32[]{:T(128)} %get-tuple-element.1679, f32[]{:T(128)} %get-tuple-element.1678, f32[]{:T(128)} %get-tuple-element.1677, ...), kind=kLoop, calls=%fused_computation.20.clone.1 | loop fusion | flops 10977280 | bytes 3293272 | tf_op jit(solution)/shard_map/while/body/eval_jaxpr/mul | solution.py:33
  254.4 7.3 %add_multiply_fusion.7 = f32[1,1024,268]{2,1,0:T(8,128)S(1)} fusion(f32[1,1024,268]{2,1,0:T(8,128)S(1)} %get-tuple-element.1530, f32[]{:T(128)} %get-tuple-element.1688, f32[]{:T(128)} %get-tuple-element.1687, f32[]{:T(128)} %get-tuple-element.1686, f32[]{:T(128)} %get-tuple-element.1685, f32[]{:T(128)} %get-tuple-element.1684, ...), kind=kLoop, calls=%fused_computation.19.clone.1 | loop fusion | flops 10977280 | bytes 3293272 | tf_op jit(solution)/shard_map/while/body/eval_jaxpr/mul | solution.py:34
  280.6 8.4 %add_multiply_fusion.6 = (f32[1,1024,268]{2,1,0:T(8,128)S(1)}, f32[1,1024,268]{2,1,0:T(8,128)S(1)}) fusion(f32[]{:T(128)} %get-tuple-element.1674, f32[]{:T(128)} %get-tuple-element.1673, f32[]{:T(128)} %get-tuple-element.1672, f32[]{:T(128)} %get-tuple-element.1671, f32[]{:T(128)} %get-tuple-element.1670, f32[]{:T(128)} %get-tuple-element.1669, ...), kind=kLoop, calls=%fused_computation.21.clone.1 | loop fusion | flops 17289216 | bytes 6586488 | tf_op jit(solution)/shard_map/while/body/eval_jaxpr/mul | solution.py:32
  296.2 7.3 %add_multiply_fusion.7 = f32[1,1024,268]{2,1,0:T(8,128)S(1)} fusion(f32[1,1024,268]{2,1,0:T(8,128)S(1)} %get-tuple-element.1530, f32[]{:T(128)} %get-tuple-element.1688, f32[]{:T(128)} %get-tuple-element.1687, f32[]{:T(128)} %get-tuple-element.1686, f32[]{:T(128)} %get-tuple-element.1685, f32[]{:T(128)} %get-tuple-element.1684, ...), kind=kLoop, calls=%fused_computation.19.clone.1 | loop fusion | flops 10977280 | bytes 3293272 | tf_op jit(solution)/shard_map/while/body/eval_jaxpr/mul | solution.py:34
  322.4 8.4 %add_multiply_fusion.6 = (f32[1,1024,268]{2,1,0:T(8,128)S(1)}, f32[1,1024,268]{2,1,0:T(8,128)S(1)}) fusion(f32[]{:T(128)} %get-tuple-element.1674, f32[]{:T(128)} %get-tuple-element.1673, f32[]{:T(128)} %get-tuple-element.1672, f32[]{:T(128)} %get-tuple-element.1671, f32[]{:T(128)} %get-tuple-element.1670, f32[]{:T(128)} %get-tuple-element.1669, ...), kind=kLoop, calls=%fused_computation.21.clone.1 | loop fusion | flops 17289216 | bytes 6586488 | tf_op jit(solution)/shard_map/while/body/eval_jaxpr/mul | solution.py:32
  337.9 7.3 %add_multiply_fusion.7 = f32[1,1024,268]{2,1,0:T(8,128)S(1)} fusion(f32[1,1024,268]{2,1,0:T(8,128)S(1)} %get-tuple-element.1530, f32[]{:T(128)} %get-tuple-element.1688, f32[]{:T(128)} %get-tuple-element.1687, f32[]{:T(128)} %get-tuple-element.1686, f32[]{:T(128)} %get-tuple-element.1685, f32[]{:T(128)} %get-tuple-element.1684, ...), kind=kLoop, calls=%fused_computation.19.clone.1 | loop fusion | flops 10977280 | bytes 3293272 | tf_op jit(solution)/shard_map/while/body/eval_jaxpr/mul | solution.py:34
  364.1 8.4 %add_multiply_fusion.6 = (f32[1,1024,268]{2,1,0:T(8,128)S(1)}, f32[1,1024,268]{2,1,0:T(8,128)S(1)}) fusion(f32[]{:T(128)} %get-tuple-element.1674, f32[]{:T(128)} %get-tuple-element.1673, f32[]{:T(128)} %get-tuple-element.1672, f32[]{:T(128)} %get-tuple-element.1671, f32[]{:T(128)} %get-tuple-element.1670, f32[]{:T(128)} %get-tuple-element.1669, ...), kind=kLoop, calls=%fused_computation.21.clone.1 | loop fusion | flops 17289216 | bytes 6586488 | tf_op jit(solution)/shard_map/while/body/eval_jaxpr/mul | solution.py:32
  372.5 7.1 %add_multiply_fusion.8 = f32[1,1024,268]{2,1,0:T(8,128)S(1)} fusion(f32[1,1024,268]{2,1,0:T(8,128)S(1)} %get-tuple-element.1530, f32[]{:T(128)} %get-tuple-element.1681, f32[]{:T(128)} %get-tuple-element.1680, f32[]{:T(128)} %get-tuple-element.1679, f32[]{:T(128)} %get-tuple-element.1678, f32[]{:T(128)} %get-tuple-element.1677, ...), kind=kLoop, calls=%fused_computation.20.clone.1 | loop fusion | flops 10977280 | bytes 3293272 | tf_op jit(solution)/shard_map/while/body/eval_jaxpr/mul | solution.py:33
  379.7 7.3 %add_multiply_fusion.7 = f32[1,1024,268]{2,1,0:T(8,128)S(1)} fusion(f32[1,1024,268]{2,1,0:T(8,128)S(1)} %get-tuple-element.1530, f32[]{:T(128)} %get-tuple-element.1688, f32[]{:T(128)} %get-tuple-element.1687, f32[]{:T(128)} %get-tuple-element.1686, f32[]{:T(128)} %get-tuple-element.1685, f32[]{:T(128)} %get-tuple-element.1684, ...), kind=kLoop, calls=%fused_computation.19.clone.1 | loop fusion | flops 10977280 | bytes 3293272 | tf_op jit(solution)/shard_map/while/body/eval_jaxpr/mul | solution.py:34
  413.5 44.8 %all-to-all-done = f32[4,8,4,32,256]{4,3,1,0,2:T(8,128)} async-done(((f32[4,8,4,32,256]{4,3,1,0,2:T(8,128)}), f32[4,8,4,32,256]{4,3,1,0,2:T(8,128)}, u32[]{:S(2)}, u32[]{:S(2)}) %all-to-all-start) | async-done | bytes 4194336 | tf_op jit(solution)/shard_map/all_to_all | solution.py:87
  463.1 30.1 %all_to_all.20 = f32[4,8,32,256]{3,2,0,1:T(8,128)S(1)} all-to-all(f32[4,8,32,256]{3,2,0,1:T(8,128)S(1)} %copy.25), channel_id=1, replica_groups=mesh['bx'=8,'bz'=4] {'bx'}, dimensions={1} | all-to-all | bytes 2097152 | tf_op jit(solution)/shard_map/all_to_all | solution.py:90
  (172 shorter events, 212.5 us)
Async XLA Ops:
  0.0 410.3 %copy-start = (s32[8,4]{0,1:T(4,128)S(1)}, s32[8,4]{0,1:T(4,128)}, u32[]{:S(2)}) copy-start(s32[8,4]{0,1:T(4,128)} %param.12) | copy-start | bytes 388
  9.0 12.4 %copy-start.4 = (f32[8,3]{0,1:T(4,128)S(1)}, f32[8,3]{0,1:T(4,128)}, u32[]{:S(2)}) copy-start(f32[8,3]{0,1:T(4,128)} %param.10) | copy-start | bytes 292
  9.0 35.3 %copy-start.7 = (s32[8]{0:T(128)S(1)}, s32[8]{0:T(128)}, u32[]{:S(2)}) copy-start(s32[8]{0:T(128)} %param.9) | copy-start | bytes 100
  9.0 44.7 %copy-start.5 = (f32[8]{0:T(128)S(1)}, f32[8]{0:T(128)}, u32[]{:S(2)}) copy-start(f32[8]{0:T(128)} %param.11) | copy-start | bytes 100
  9.0 58.9 %copy-start.6 = (s32[1,1,2]{2,1,0:T(1,128)S(1)}, s32[1,1,2]{2,1,0:T(1,128)}, u32[]{:S(2)}) copy-start(s32[1,1,2]{2,1,0:T(1,128)} %param.13) | copy-start | bytes 28
  16.3 53.6 %collective-permute-start = (bf16[4,8,1024,12]{2,1,3,0:T(8,128)(2,1)S(1)}, bf16[4,8,1024,12]{2,1,3,0:T(8,128)(2,1)S(1)}, u32[]{:S(2)}, u32[]{:S(2)}) collective-permute-start(bf16[4,8,1024,12]{2,1,3,0:T(8,128)(2,1)S(1)} %copy.33), channel_id=1, source_target_pairs={{0,4},{4,8},{8,12},{12,16},{16,20},{20,24},{24,28},{1,5},{5,9},{9,... | collective-permute-start | bytes 2359304 | tf_op jit(solution)/shard_map/ppermute | solution.py:12
  69.9 2.0 copy-start.2
  101.1 2.8 copy-start.1
  103.9 4.3 copy-start.3
  139.3 4.0 copy-start.1
  143.4 6.5 %copy-start.3 = (bf16[4,8,1024,12]{2,1,3,0:T(8,128)(2,1)S(1)}, bf16[4,8,1024,12]{2,1,3,0:T(8,128)(2,1)}, u32[]{:S(2)}) copy-start(bf16[4,8,1024,12]{2,1,3,0:T(8,128)(2,1)} %copy-done.2) | copy-start | bytes 2359300 | tf_op jit(solution)/shard_map/while
  181.1 4.0 copy-start.1
  185.1 6.5 %copy-start.3 = (bf16[4,8,1024,12]{2,1,3,0:T(8,128)(2,1)S(1)}, bf16[4,8,1024,12]{2,1,3,0:T(8,128)(2,1)}, u32[]{:S(2)}) copy-start(bf16[4,8,1024,12]{2,1,3,0:T(8,128)(2,1)} %copy-done.2) | copy-start | bytes 2359300 | tf_op jit(solution)/shard_map/while
  222.8 4.0 copy-start.1
  226.9 6.5 %copy-start.3 = (bf16[4,8,1024,12]{2,1,3,0:T(8,128)(2,1)S(1)}, bf16[4,8,1024,12]{2,1,3,0:T(8,128)(2,1)}, u32[]{:S(2)}) copy-start(bf16[4,8,1024,12]{2,1,3,0:T(8,128)(2,1)} %copy-done.2) | copy-start | bytes 2359300 | tf_op jit(solution)/shard_map/while
  264.6 4.0 copy-start.1
  268.6 6.5 %copy-start.3 = (bf16[4,8,1024,12]{2,1,3,0:T(8,128)(2,1)S(1)}, bf16[4,8,1024,12]{2,1,3,0:T(8,128)(2,1)}, u32[]{:S(2)}) copy-start(bf16[4,8,1024,12]{2,1,3,0:T(8,128)(2,1)} %copy-done.2) | copy-start | bytes 2359300 | tf_op jit(solution)/shard_map/while
  306.3 4.0 copy-start.1
  310.4 6.5 %copy-start.3 = (bf16[4,8,1024,12]{2,1,3,0:T(8,128)(2,1)S(1)}, bf16[4,8,1024,12]{2,1,3,0:T(8,128)(2,1)}, u32[]{:S(2)}) copy-start(bf16[4,8,1024,12]{2,1,3,0:T(8,128)(2,1)} %copy-done.2) | copy-start | bytes 2359300 | tf_op jit(solution)/shard_map/while
  348.1 4.0 copy-start.1
  352.1 6.5 %copy-start.3 = (bf16[4,8,1024,12]{2,1,3,0:T(8,128)(2,1)S(1)}, bf16[4,8,1024,12]{2,1,3,0:T(8,128)(2,1)}, u32[]{:S(2)}) copy-start(bf16[4,8,1024,12]{2,1,3,0:T(8,128)(2,1)} %copy-done.2) | copy-start | bytes 2359300 | tf_op jit(solution)/shard_map/while
  389.8 4.0 copy-start.1
  393.9 6.5 %copy-start.3 = (bf16[4,8,1024,12]{2,1,3,0:T(8,128)(2,1)S(1)}, bf16[4,8,1024,12]{2,1,3,0:T(8,128)(2,1)}, u32[]{:S(2)}) copy-start(bf16[4,8,1024,12]{2,1,3,0:T(8,128)(2,1)} %copy-done.2) | copy-start | bytes 2359300 | tf_op jit(solution)/shard_map/while
  405.2 53.0 %all-to-all-start = ((f32[4,8,4,32,256]{4,3,1,0,2:T(8,128)}), f32[4,8,4,32,256]{4,3,1,0,2:T(8,128)}, u32[]{:S(2)}, u32[]{:S(2)}) async-start(f32[4,8,4,32,256]{4,3,1,0,2:T(8,128)} %copy.20), calls=%async_computation | async-start | bytes 8388608 | tf_op jit(solution)/shard_map/all_to_all | solution.py:87
  (7 other events, 14.1 us)
where the time goes:
time: 498 us; the launch traced here: 495 us
  other arithmetic  297 us (60%)
  local copies, waits for them, and re-layouts  68.7 us (14%)
  waiting for transfers between devices  44.8 us (9%)
  between operations  43.9 us (9%)
  blocking collectives  30.1 us (6%)
  starting transfers between devices  10.2 us (2%)
    mul x8, other arithmetic, classify(): alpha * lookup(tf_color[:, 0])  67.3 us
    mul x8, other arithmetic, classify(): alpha * lookup(tf_color[:, 2])  58.1 us
    mul x8, other arithmetic, classify(): alpha * lookup(tf_color[:, 1])  57.1 us
    add x8, other arithmetic, advance(): return acc + (1.0 - acc[3:4]) * ((1.0 - frac) * near + frac * far)  49.9 us
    all_to_all x1, waiting for transfers between devices, per_device(): lax.all_to_all(pieces, 'bz', split_axis=2, concat_axis=2, tiled=True)  44.8 us
    all_to_all x1, blocking collectives, per_device(): lax.all_to_all(merged, 'bx', split_axis=1, concat_axis=3, tiled=True)  30.1 us
    mul x8, other arithmetic, advance(): classify(raw, breakpoints, tf_color, tf_opacity)  22.9 us
    while x8, other arithmetic  19.5 us
  transfers between devices with their start and end apart: 2, of which 1 were waited for; matrix products, arithmetic and copies ran while one was open for 2% of the time, Pallas kernels for 0%

commit v1 on v0

v1 whole, which is shorter than its diff:
```python
import functools

import jax
import jax.numpy as jnp
from jax import lax
from jax.experimental import pallas as pl
from jax.experimental.pallas import tpu as pltpu
from jax.sharding import PartitionSpec as P

LANES = 128
SUB = 16
LOG2E = 1.4426950408889634
CODE = 65535.0


def encode(value):
    root = jnp.sqrt(jnp.sqrt(jnp.maximum(value, 0.0)))
    return jnp.round(root * CODE - 32768.0).astype(jnp.int32).astype(jnp.int16)


def decode(code):
    root = (code.astype(jnp.int32).astype(jnp.float32) + 32768.0) * (1.0 / CODE)
    square = root * root
    return square * square


def halo_pitch(reach):
    pitch = 16
    while pitch < reach:
        pitch *= 2
    return pitch


def pack_kernel(pitch, src_ref, dst_ref):
    slices = src_ref.shape[1]
    per = LANES // pitch
    lane = lax.broadcasted_iota(jnp.int32, (src_ref.shape[2], LANES), 1)
    for f in range(src_ref.shape[0]):
        for v in range(dst_ref.shape[2] // LANES):
            total = jnp.zeros((src_ref.shape[2], LANES), jnp.float32)
            for s in range(per):
                k = v * per + s
                if k < slices:
                    x = src_ref[f, k].astype(jnp.float32)
                    x = pltpu.roll(x, (s + 1) * pitch % LANES, 1)
                    slot = (lane >= s * pitch) & (lane < (s + 1) * pitch)
                    total = jnp.where(slot, x, total)
            dst_ref[f, :, v * LANES : (v + 1) * LANES] = total.astype(jnp.bfloat16)


def pack_halo(fields, pitch):
    nf, slices, height, width = fields.shape
    rows = 128
    lanes = -(-slices * pitch // LANES) * LANES
    return pl.pallas_call(
        functools.partial(pack_kernel, pitch),
        grid=(height // rows,),
        in_specs=[pl.BlockSpec((nf, slices, rows, LANES), lambda r: (0, 0, r, width // LANES - 1))],
        out_specs=pl.BlockSpec((nf, rows, lanes), lambda r: (0, r, 0)),
        out_shape=jax.ShapeDtypeStruct((nf, height, lanes), jnp.bfloat16),
        name="pack_halo",
    )(fields)


def build_tables(marks_ref, color_ref, opacity_ref, tab_ref):
    nbp = marks_ref.shape[0]
    lane = lax.broadcasted_iota(jnp.int32, (SUB, LANES), 1)

    def spread(value):
        total = jnp.zeros((SUB, LANES), jnp.float32)
        for j in range(nbp - 1):
            total = jnp.where(lane == j, value(j), total)
        return total

    mark = lambda j: marks_ref[j].astype(jnp.float32)
    start = spread(mark)
    step = jnp.where(lane < nbp - 1, spread(lambda j: mark(j + 1)) - start, 1.0)
    for q in range(4):
        value = (lambda j: color_ref[3 * j + q]) if q < 3 else (lambda j: opacity_ref[j])
        first = spread(value)
        slope = (spread(lambda j: value(j + 1)) - first) / step
        base = first - slope * start
        scale = 1.0 if q < 3 else -LOG2E
        tab_ref[2 * q] = base * scale
        tab_ref[2 * q + 1] = slope * scale


def make_classify(marks_ref, tab_ref):
    nbp = marks_ref.shape[0]
    marks = [marks_ref[j].astype(jnp.float32) for j in range(nbp)]
    rows_of = lambda q: tab_ref[q]

    def look(q, seg):
        return jnp.take_along_axis(rows_of(q), seg, axis=1, mode="promise_in_bounds")

    def classify(raw):
        x0, x1, x2, x3 = [r.astype(jnp.float32) for r in raw]
        level = 127.5 * jnp.tanh(0.5 * x0) + 127.5
        swirl = x1 * x1 + x2 * x2 + x3 * x3
        seg = jnp.zeros(level.shape, jnp.int32)
        for j in range(1, nbp - 1):
            seg = jnp.where(level >= marks[j], j, seg)
        rate = look(6, seg) + look(7, seg) * level
        alpha = 1.0 - jnp.exp2(rate * (0.25 + swirl))
        return [alpha * (look(2 * q, seg) + look(2 * q + 1, seg) * level) for q in range(3)] + [alpha]

    return classify


def turn(parts, shift, lane):
    rolled = [pltpu.roll(p, shift, 1) for p in parts]
    return [jnp.where(lane < shift, rolled[i - 1], rolled[i]) for i in range(len(parts))]


def turn_back(parts, lane):
    rolled = [pltpu.roll(p, LANES - 1, 1) for p in parts]
    n = len(parts)
    return [jnp.where(lane == LANES - 1, rolled[(i + 1) % n], rolled[i]) for i in range(n)]


def volume_kernel(pitch, marks_ref, color_ref, opacity_ref, live_ref, fields_ref, halo_ref, out_ref, tab_ref):
    nf, slices, rows, width = fields_ref.shape
    nv = width // LANES
    per = LANES // pitch
    step = pl.program_id(0)

    @pl.when(step == 0)
    def _():
        build_tables(marks_ref, color_ref, opacity_ref, tab_ref)

    low = live_ref[0]
    high = live_ref[1]
    row0 = step * rows
    alive = (row0 < high) & (row0 + rows > low)
    edge = jnp.where(lax.axis_index("bx") > 0, 1.0, 0.0).astype(jnp.float32)
    base = 3 * (lax.axis_index("bz") * slices) // 8

    @pl.when(jnp.logical_not(alive))
    def _():
        out_ref[...] = jnp.full(out_ref.shape, -32768, jnp.int16)

    @pl.when(alive)
    def _():
        lane = lax.broadcasted_iota(jnp.int32, (SUB, LANES), 1)
        sub = lax.broadcasted_iota(jnp.int32, (SUB, LANES), 0)
        classify = make_classify(marks_ref, tab_ref)

        def group(g, carry):
            at = pl.ds(pl.multiple_of(g * SUB, SUB), SUB)
            halo = []
            for v in range(halo_ref.shape[2] // LANES):
                s = classify([halo_ref[f, at, v * LANES : (v + 1) * LANES] for f in range(nf)])
                halo.append([c * edge for c in s])
            color = [[jnp.zeros((SUB, LANES), jnp.float32) for _ in range(nv)] for _ in range(3)]
            clear = [jnp.ones((SUB, LANES), jnp.float32) for _ in range(nv)]
            for k in range(slices):
                whole = 3 * k // 8
                frac = (3 * k % 8) / 8.0
                if k > 0 and whole > 3 * (k - 1) // 8:
                    color = [turn_back(c, lane) for c in color]
                    clear = turn_back(clear, lane)
                a = base + whole
                by_part = [
                    classify([fields_ref[f, k, at, v * LANES : (v + 1) * LANES] for f in range(nf)])
                    for v in range(nv)
                ]
                sheared = []
                for q in range(4):
                    parts = [by_part[v][q] for v in range(nv)]
                    held = halo[k // per][q]
                    to = (LANES - (k % per + 1) * pitch) % LANES
                    near_halo = pltpu.roll(held, to, 1) if to else held
                    parts[-1] = jnp.where(lane >= LANES - a, near_halo, parts[-1])
                    if frac > 0:
                        far = turn(parts, 1, lane)
                        far_halo = pltpu.roll(held, to + 1, 1)
                        spot = jnp.where(a == 0, 0, LANES - a)
                        first = (lane == spot) & (a == 0)
                        last = (lane == spot) & (a > 0)
                        far[0] = jnp.where(first, far_halo, far[0])
                        far[-1] = jnp.where(last, far_halo, far[-1])
                        parts = [p + frac * (r - p) for p, r in zip(parts, far)]
                    sheared.append(parts)
                for q in range(3):
                    color[q] = [c + t * s for c, t, s in zip(color[q], clear, sheared[q])]
                clear = [t - t * s for t, s in zip(clear, sheared[3])]
            end = base + 3 * (slices - 1) // 8
            row = row0 + g * SUB + sub
            keep = (row >= low) & (row < high)
            for q in range(4):
                parts = color[q] if q < 3 else [1.0 - t for t in clear]
                parts = turn(parts, end, lane)
                for v in range(nv):
                    out_ref[0, q, 0, at, v * LANES : (v + 1) * LANES] = encode(jnp.where(keep, parts[v], 0.0))
            return carry

        lax.fori_loop(0, rows // SUB, group, 0)


def volume(fields, halo, breakpoints, tf_color, tf_opacity, live, pitch, count_x, count_z):
    nf, slices, height, width = fields.shape
    assert slices % 8 == 0
    owned = height // (count_x * count_z)
    smem = pl.BlockSpec(memory_space=pltpu.SMEM)
    return pl.pallas_call(
        functools.partial(volume_kernel, pitch),
        grid=(count_x * count_z,),
        in_specs=[
            smem,
            smem,
            smem,
            smem,
            pl.BlockSpec((nf, slices, owned, width), lambda r: (0, 0, r, 0)),
            pl.BlockSpec((nf, owned, halo.shape[2]), lambda r: (0, r, 0)),
        ],
        out_specs=pl.BlockSpec((1, 4, 1, owned, width), lambda r: (r % count_z, 0, r // count_z, 0, 0)),
        out_shape=jax.ShapeDtypeStruct((count_z, 4, count_x, owned, width), jnp.int16),
        scratch_shapes=[pltpu.VMEM((8, SUB, LANES), jnp.float32)],
        name="volume",
    )(breakpoints, tf_color.reshape(-1), tf_opacity, live, fields, halo)


def merge_kernel(order_ref, src_ref, dst_ref):
    depth = src_ref.shape[0]
    column = lax.axis_index("bx")
    rows = src_ref.shape[3]
    for g in range(0, rows, SUB):
        at = slice(g, g + SUB)
        total = None
        for k in range(depth):
            d = order_ref[column * depth + k]
            part = [decode(src_ref[d, q, 0, at]) for q in range(4)]
            if total is None:
                total = part
            else:
                clear = 1.0 - total[3]
                total = [t + clear * p for t, p in zip(total, part)]
        for q in range(4):
            dst_ref[0, q, at] = encode(total[q])


def merge(arrived, order):
    depth, _, count_x, owned, width = arrived.shape
    return pl.pallas_call(
        merge_kernel,
        grid=(count_x,),
        in_specs=[
            pl.BlockSpec(memory_space=pltpu.SMEM),
            pl.BlockSpec((depth, 4, 1, owned, width), lambda i: (0, 0, i, 0, 0)),
        ],
        out_specs=pl.BlockSpec((1, 4, owned, width), lambda i: (i, 0, 0, 0)),
        out_shape=jax.ShapeDtypeStruct((count_x, 4, owned, width), jnp.int16),
        name="merge",
    )(order.reshape(-1), arrived)


def open_kernel(src_ref, dst_ref):
    dst_ref[...] = decode(src_ref[0])


def open_image(moved):
    count_x, _, owned, width = moved.shape
    return pl.pallas_call(
        open_kernel,
        grid=(count_x,),
        in_specs=[pl.BlockSpec((1, 4, owned, width), lambda i: (i, 0, 0, 0))],
        out_specs=pl.BlockSpec((4, owned, width), lambda i: (0, 0, i)),
        out_shape=jax.ShapeDtypeStruct((4, owned, count_x * width), jnp.float32),
        name="open_image",
    )(moved)


def per_device(fields, breakpoints, tf_color, tf_opacity, depth_order, live_rows):
    slices = fields.shape[1]
    count_x = lax.axis_size("bx")
    count_z = lax.axis_size("bz")
    reach = 3 * (slices * count_z - 1) // 8 + 1
    pitch = halo_pitch(reach)
    rim = pack_halo(fields, pitch)
    halo = lax.ppermute(rim, "bx", [(i, i + 1) for i in range(count_x - 1)])
    live = live_rows.reshape(2)
    partial = volume(fields, halo, breakpoints, tf_color, tf_opacity, live, pitch, count_x, count_z)
    arrived = lax.all_to_all(partial, "bz", split_axis=0, concat_axis=0, tiled=True)
    merged = merge(arrived, depth_order)
    moved = lax.all_to_all(merged, "bx", split_axis=0, concat_axis=0, tiled=True)
    return open_image(moved)


def solution(mesh):
    return jax.shard_map(
        per_device,
        mesh=mesh,
        in_specs=(P(None, "bz", None, "bx"), P(), P(), P(), P(), P("bx", "bz", None)),
        out_specs=P(None, ("bx", "bz"), None),
        check_vma=False,
    )
```

time: 498 us -> 249 us (0.50)
  other arithmetic: 297 us -> 0 us
  Pallas kernels: 0 us -> 105 us
  local copies, waits for them, and re-layouts: 68.7 us -> 3.81 us
  between operations: 43.9 us -> 0.03 us
  starting transfers between devices: 10.2 us -> 41.1 us
  blocking collectives: 30.1 us -> 51.5 us
    mul x44 -> x0, other arithmetic: 209 us -> none  [the longest x8 67.3 us: classify(): alpha * lookup(tf_color[:, 0])]
    pallas_call x0 -> x4, Pallas kernels: none -> 105 us  [the longest x1 85.6 us: volume(): pl.pallas_call(functools.partial(volume_kernel, pitch), grid=(count_x * c...]
    add x11 -> x0, other arithmetic: 50.6 us -> none  [the longest x8 49.9 us: advance(): return acc + (1.0 - acc[3:4]) * ((1.0 - frac) * near + frac * far)]
    all_to_all x1, starting transfers between devices: 5.06 us -> 36.1 us  [per_device(): lax.all_to_all(partial, 'bz', split_axis=0, concat_axis=0, tiled=True)]
    slice x23 -> x0, local copies, waits for them, and re-layouts: 23.1 us -> none  [the longest x1 9.01 us: per_device(): rim = from_behind(fields[:, :, :, width - reach:], 'bx', 1)]
    ppermute x1, waiting for transfers between devices: 0.01 us -> 21.9 us  [per_device(): halo = lax.ppermute(rim, 'bx', [(i, i + 1) for i in range(count_x - 1)])]
    all_to_all x1, blocking collectives: 30.1 us -> 51.5 us  [per_device(): lax.all_to_all(merged, 'bx', split_axis=0, concat_axis=0, tiled=True)]
    all_to_all x1, waiting for transfers between devices: 44.8 us -> 24.9 us  [per_device(): lax.all_to_all(partial, 'bz', split_axis=0, concat_axis=0, tiled=True)]
  transfers between devices with their start and end apart: 2 -> 2, of which waited for: 1 -> 2; matrix products, arithmetic and copies ran while one was open for 2% -> 1% of each run, Pallas kernels for 0% -> 0%
where the time goes in v1:
time: 249 us; the launch traced here: 248 us
  Pallas kernels  105 us (42%)
  blocking collectives  51.5 us (21%)
  waiting for transfers between devices  46.8 us (19%)
  starting transfers between devices  41.1 us (17%)
  local copies, waits for them, and re-layouts  3.81 us (2%)
    pallas_call x1, Pallas kernels, volume(): pl.pallas_call(functools.partial(volume_kernel, pitch), grid=(count_x * c...  85.6 us
    all_to_all x1, blocking collectives, per_device(): lax.all_to_all(merged, 'bx', split_axis=0, concat_axis=0, tiled=True)  51.5 us
    all_to_all x1, starting transfers between devices, per_device(): lax.all_to_all(partial, 'bz', split_axis=0, concat_axis=0, tiled=True)  36.1 us
    all_to_all x1, waiting for transfers between devices, per_device(): lax.all_to_all(partial, 'bz', split_axis=0, concat_axis=0, tiled=True)  24.9 us
    ppermute x1, waiting for transfers between devices, per_device(): halo = lax.ppermute(rim, 'bx', [(i, i + 1) for i in range(count_x - 1)])  21.9 us
    pallas_call x1, Pallas kernels, pack_halo(): pl.pallas_call(functools.partial(pack_kernel, pitch), grid=(height // row...  7.84 us
    pallas_call x1, Pallas kernels, merge(): pl.pallas_call(merge_kernel, grid=(count_x,), in_specs=[pl.BlockSpec(memo...  6.17 us
  transfers between devices with their start and end apart: 2, of which 2 were waited for; matrix products, arithmetic and copies ran while one was open for 1% of the time, Pallas kernels for 0%

profile of v1, /device:TPU:0, one launch (start us, length us, event | category | flops | bytes accessed | tf_op | source)
XLA Modules:
  0.0 247.7 jit_solution(16395172172148917632)
XLA Ops:
  0.0 0.0 copy-start.2
  0.0 7.8 %pack_halo.1 = bf16[4,1024,128]{2,1,0:T(8,128)(2,1)} custom-call(bf16[4,8,1024,256]{3,2,1,0:T(8,128)(2,1)} %fields_ref.1), custom_call_target="tpu_custom_call" | custom-call | tf_op jit(solution)/shard_map/pack_halo/pallas_call | solution.py:55
  7.8 4.9 %collective-permute-start = (bf16[4,1024,128]{2,1,0:T(8,128)(2,1)}, bf16[4,1024,128]{2,1,0:T(8,128)(2,1)S(1)}, u32[]{:S(2)}, u32[]{:S(2)}) collective-permute-start(bf16[4,1024,128]{2,1,0:T(8,128)(2,1)} %pack_halo.1), channel_id=1, source_target_pairs={{0,4},{4,8},{8,12},{12,16},{16,20},{20,24},{24,28},{1,5},{5,9},{9,... | collective-permute-start | bytes 3145736 | tf_op jit(solution)/shard_map/ppermute | solution.py:280
  12.8 0.0 copy-done.2
  12.8 0.1 copy.10
  12.9 0.7 reshape.10.color_ref
  13.5 21.9 %collective-permute-done.halo_ref = bf16[4,1024,128]{2,1,0:T(8,128)(2,1)S(1)} collective-permute-done((bf16[4,1024,128]{2,1,0:T(8,128)(2,1)}, bf16[4,1024,128]{2,1,0:T(8,128)(2,1)S(1)}, u32[]{:S(2)}, u32[]{:S(2)}) %collective-permute-start) | collective-permute-done | bytes 1048608 | tf_op jit(solution)/shard_map/ppermute | solution.py:280
  35.4 0.0 copy-start.1
  35.4 1.0 copy-done.1
  36.4 85.6 %volume.1 = s16[4,4,8,32,256]{4,3,2,1,0:T(8,128)(2,1)} custom-call(s32[8]{0:T(128)} %marks_ref.1, f32[24]{0:T(128)} %reshape.10.color_ref, f32[8]{0:T(128)} %opacity_ref.1, s32[2]{0:T(128)} %bitcast.1, bf16[4,8,1024,256]{3,2,1,0:T(8,128)(2,1)} %fields_ref.1, bf16[4,1024,128]{2,1,0:T(8,128)(2,1)} %copy-done.1), custom_call_target="tpu_custom_call" | custom-call | tf_op jit(solution)/shard_map/volume/pallas_call | solution.py:205
  122.0 0.0 copy-start.3
  122.0 36.1 %all-to-all-start = ((s16[4,4,8,32,256]{4,3,2,1,0:T(8,128)(2,1)}), s16[4,4,8,32,256]{4,3,2,1,0:T(8,128)(2,1)S(1)}, u32[]{:S(2)}, u32[]{:S(2)}) async-start(s16[4,4,8,32,256]{4,3,2,1,0:T(8,128)(2,1)} %volume.1), calls=%async_computation | async-start | bytes 4194304 | tf_op jit(solution)/shard_map/all_to_all | solution.py:283
  158.1 0.0 copy-done.3
  158.1 0.1 copy.9
  158.2 0.7 reshape.9.order_ref
  158.8 24.9 %all-to-all-done.src_ref = s16[4,4,8,32,256]{4,3,2,1,0:T(8,128)(2,1)S(1)} async-done(((s16[4,4,8,32,256]{4,3,2,1,0:T(8,128)(2,1)}), s16[4,4,8,32,256]{4,3,2,1,0:T(8,128)(2,1)S(1)}, u32[]{:S(2)}, u32[]{:S(2)}) %all-to-all-start) | async-done | bytes 2097184 | tf_op jit(solution)/shard_map/all_to_all | solution.py:283
  183.8 0.0 copy-start
  183.8 1.4 copy-done
  185.1 6.2 %merge.1 = s16[8,4,32,256]{3,2,1,0:T(8,128)(2,1)} custom-call(s32[32]{0:T(128)} %reshape.9.order_ref, s16[4,4,8,32,256]{4,3,2,1,0:T(8,128)(2,1)} %copy-done), custom_call_target="tpu_custom_call" | custom-call | tf_op jit(solution)/shard_map/merge/pallas_call | solution.py:244
  191.3 51.5 %all_to_all.10.src_ref = s16[8,4,32,256]{3,2,1,0:T(8,128)(2,1)} all-to-all(s16[8,4,32,256]{3,2,1,0:T(8,128)(2,1)} %merge.1), channel_id=1, replica_groups=mesh['bx'=8,'bz'=4] {'bx'}, dimensions={0} | all-to-all | bytes 1048576 | tf_op jit(solution)/shard_map/all_to_all | solution.py:285
  242.8 4.9 %open_image.1 = f32[4,32,2048]{2,1,0:T(8,128)} custom-call(s16[8,4,32,256]{3,2,1,0:T(8,128)(2,1)} %all_to_all.10.src_ref), custom_call_target="tpu_custom_call" | custom-call | tf_op jit(solution)/shard_map/open_image/pallas_call | solution.py:263
Async XLA Ops:
  0.0 12.8 %copy-start.2 = (f32[8,3]{0,1:T(4,128)S(1)}, f32[8,3]{0,1:T(4,128)}, u32[]{:S(2)}) copy-start(f32[8,3]{0,1:T(4,128)} %param.8) | copy-start | bytes 292
  7.8 27.6 %collective-permute-start = (bf16[4,1024,128]{2,1,0:T(8,128)(2,1)}, bf16[4,1024,128]{2,1,0:T(8,128)(2,1)S(1)}, u32[]{:S(2)}, u32[]{:S(2)}) collective-permute-start(bf16[4,1024,128]{2,1,0:T(8,128)(2,1)} %pack_halo.1), channel_id=1, source_target_pairs={{0,4},{4,8},{8,12},{12,16},{16,20},{20,24},{24,28},{1,5},{5,9},{9,... | collective-permute-start | bytes 3145736 | tf_op jit(solution)/shard_map/ppermute | solution.py:280
  35.4 1.0 copy-start.1
  122.0 36.1 %copy-start.3 = (s32[8,4]{0,1:T(4,128)S(1)}, s32[8,4]{0,1:T(4,128)}, u32[]{:S(2)}) copy-start(s32[8,4]{0,1:T(4,128)} %param.10) | copy-start | bytes 388
  122.0 61.8 %all-to-all-start = ((s16[4,4,8,32,256]{4,3,2,1,0:T(8,128)(2,1)}), s16[4,4,8,32,256]{4,3,2,1,0:T(8,128)(2,1)S(1)}, u32[]{:S(2)}, u32[]{:S(2)}) async-start(s16[4,4,8,32,256]{4,3,2,1,0:T(8,128)(2,1)} %volume.1), calls=%async_computation | async-start | bytes 4194304 | tf_op jit(solution)/shard_map/all_to_all | solution.py:283
  183.8 1.4 copy-start

commit v2 on v1

--- a/solution.py
+++ b/solution.py
@@ -64,10 +64,10 @@
 
 def build_tables(marks_ref, color_ref, opacity_ref, tab_ref):
     nbp = marks_ref.shape[0]
-    lane = lax.broadcasted_iota(jnp.int32, (SUB, LANES), 1)
+    lane = lax.broadcasted_iota(jnp.int32, (8, LANES), 0)
 
     def spread(value):
-        total = jnp.zeros((SUB, LANES), jnp.float32)
+        total = jnp.zeros((8, LANES), jnp.float32)
         for j in range(nbp - 1):
             total = jnp.where(lane == j, value(j), total)
         return total
@@ -91,7 +91,7 @@
     rows_of = lambda q: tab_ref[q]
 
     def look(q, seg):
-        return jnp.take_along_axis(rows_of(q), seg, axis=1, mode="promise_in_bounds")
+        return jnp.concatenate([jnp.take_along_axis(rows_of(q), seg[i : i + 8], axis=0, mode="promise_in_bounds") for i in range(0, SUB, 8)], axis=0)
 
     def classify(raw):
         x0, x1, x2, x3 = [r.astype(jnp.float32) for r in raw]
@@ -169,16 +169,12 @@
                     parts = [by_part[v][q] for v in range(nv)]
                     held = halo[k // per][q]
                     to = (LANES - (k % per + 1) * pitch) % LANES
-                    near_halo = pltpu.roll(held, to, 1) if to else held
-                    parts[-1] = jnp.where(lane >= LANES - a, near_halo, parts[-1])
+                    held = pltpu.roll(held, to, 1) if to else held
+                    own = parts[-1]
+                    parts[-1] = jnp.where(lane >= LANES - a, held, own)
                     if frac > 0:
-                        far = turn(parts, 1, lane)
-                        far_halo = pltpu.roll(held, to + 1, 1)
-                        spot = jnp.where(a == 0, 0, LANES - a)
-                        first = (lane == spot) & (a == 0)
-                        last = (lane == spot) & (a > 0)
-                        far[0] = jnp.where(first, far_halo, far[0])
-                        far[-1] = jnp.where(last, far_halo, far[-1])
+                        far = parts[:-1] + [jnp.where(lane >= LANES - 1 - a, held, own)]
+                        far = turn(far, 1, lane)
                         parts = [p + frac * (r - p) for p, r in zip(parts, far)]
                     sheared.append(parts)
                 for q in range(3):
@@ -215,7 +211,7 @@
         ],
         out_specs=pl.BlockSpec((1, 4, 1, owned, width), lambda r: (r % count_z, 0, r // count_z, 0, 0)),
         out_shape=jax.ShapeDtypeStruct((count_z, 4, count_x, owned, width), jnp.int16),
-        scratch_shapes=[pltpu.VMEM((8, SUB, LANES), jnp.float32)],
+        scratch_shapes=[pltpu.VMEM((8, 8, LANES), jnp.float32)],
         name="volume",
     )(breakpoints, tf_color.reshape(-1), tf_opacity, live, fields, halo)
 

time: 249 us -> 138 us (0.55)
  Pallas kernels: 105 us -> 48.5 us
  starting transfers between devices: 41.1 us -> 12.4 us
  blocking collectives: 51.5 us -> 24 us
    pallas_call x1, Pallas kernels: 85.6 us -> 29.6 us  [volume(): pl.pallas_call(functools.partial(volume_kernel, pitch), grid=(count_x * c...]
    all_to_all x1, starting transfers between devices: 36.1 us -> 7.45 us  [per_device(): lax.all_to_all(partial, 'bz', split_axis=0, concat_axis=0, tiled=True)]
    all_to_all x1, blocking collectives: 51.5 us -> 24 us  [per_device(): lax.all_to_all(merged, 'bx', split_axis=0, concat_axis=0, tiled=True)]
where the time goes in v2:
time: 138 us; the launch traced here: 136 us
  Pallas kernels  48.5 us (35%)
  waiting for transfers between devices  47.3 us (34%)
  blocking collectives  24 us (17%)
  starting transfers between devices  12.4 us (9%)
  local copies, waits for them, and re-layouts  3.81 us (3%)
    pallas_call x1, Pallas kernels, volume(): pl.pallas_call(functools.partial(volume_kernel, pitch), grid=(count_x * c...  29.6 us
    all_to_all x1, waiting for transfers between devices, per_device(): lax.all_to_all(partial, 'bz', split_axis=0, concat_axis=0, tiled=True)  25.4 us
    all_to_all x1, blocking collectives, per_device(): lax.all_to_all(merged, 'bx', split_axis=0, concat_axis=0, tiled=True)  24 us
    ppermute x1, waiting for transfers between devices, per_device(): halo = lax.ppermute(rim, 'bx', [(i, i + 1) for i in range(count_x - 1)])  21.9 us
    pallas_call x1, Pallas kernels, pack_halo(): pl.pallas_call(functools.partial(pack_kernel, pitch), grid=(height // row...  7.84 us
    all_to_all x1, starting transfers between devices, per_device(): lax.all_to_all(partial, 'bz', split_axis=0, concat_axis=0, tiled=True)  7.45 us
    pallas_call x1, Pallas kernels, merge(): pl.pallas_call(merge_kernel, grid=(count_x,), in_specs=[pl.BlockSpec(memo...  6.17 us
    pallas_call x1, Pallas kernels, open_image(): pl.pallas_call(open_kernel, grid=(count_x,), in_specs=[pl.BlockSpec((1, 4...  4.94 us
  transfers between devices with their start and end apart: 2, of which 2 were waited for; matrix products, arithmetic and copies ran while one was open for 1% of the time, Pallas kernels for 0%

profile of v2, /device:TPU:0, one launch (start us, length us, event | category | flops | bytes accessed | tf_op | source)
XLA Modules:
  0.0 136.1 jit_solution(1901586505811554259)
XLA Ops:
  0.0 0.0 copy-start.2
  0.0 7.8 %pack_halo.1 = bf16[4,1024,128]{2,1,0:T(8,128)(2,1)} custom-call(bf16[4,8,1024,256]{3,2,1,0:T(8,128)(2,1)} %fields_ref.1), custom_call_target="tpu_custom_call" | custom-call | tf_op jit(solution)/shard_map/pack_halo/pallas_call | solution.py:55
  7.8 4.9 %collective-permute-start = (bf16[4,1024,128]{2,1,0:T(8,128)(2,1)}, bf16[4,1024,128]{2,1,0:T(8,128)(2,1)S(1)}, u32[]{:S(2)}, u32[]{:S(2)}) collective-permute-start(bf16[4,1024,128]{2,1,0:T(8,128)(2,1)} %pack_halo.1), channel_id=1, source_target_pairs={{0,4},{4,8},{8,12},{12,16},{16,20},{20,24},{24,28},{1,5},{5,9},{9,... | collective-permute-start | bytes 3145736 | tf_op jit(solution)/shard_map/ppermute | solution.py:276
  12.8 0.0 copy-done.2
  12.8 0.1 copy.10
  12.9 0.7 reshape.10.color_ref
  13.5 21.9 %collective-permute-done.halo_ref = bf16[4,1024,128]{2,1,0:T(8,128)(2,1)S(1)} collective-permute-done((bf16[4,1024,128]{2,1,0:T(8,128)(2,1)}, bf16[4,1024,128]{2,1,0:T(8,128)(2,1)S(1)}, u32[]{:S(2)}, u32[]{:S(2)}) %collective-permute-start) | collective-permute-done | bytes 1048608 | tf_op jit(solution)/shard_map/ppermute | solution.py:276
  35.4 0.0 copy-start.1
  35.4 1.0 copy-done.1
  36.4 29.6 %volume.1 = s16[4,4,8,32,256]{4,3,2,1,0:T(8,128)(2,1)} custom-call(s32[8]{0:T(128)} %marks_ref.1, f32[24]{0:T(128)} %reshape.10.color_ref, f32[8]{0:T(128)} %opacity_ref.1, s32[2]{0:T(128)} %bitcast.1, bf16[4,8,1024,256]{3,2,1,0:T(8,128)(2,1)} %fields_ref.1, bf16[4,1024,128]{2,1,0:T(8,128)(2,1)} %copy-done.1), custom_call_target="tpu_custom_call" | custom-call | tf_op jit(solution)/shard_map/volume/pallas_call | solution.py:201
  66.0 0.0 copy-start.3
  66.0 7.4 %all-to-all-start = ((s16[4,4,8,32,256]{4,3,2,1,0:T(8,128)(2,1)}), s16[4,4,8,32,256]{4,3,2,1,0:T(8,128)(2,1)S(1)}, u32[]{:S(2)}, u32[]{:S(2)}) async-start(s16[4,4,8,32,256]{4,3,2,1,0:T(8,128)(2,1)} %volume.1), calls=%async_computation | async-start | bytes 4194304 | tf_op jit(solution)/shard_map/all_to_all | solution.py:279
  73.4 0.0 copy-done.3
  73.4 0.1 copy.9
  73.5 0.7 reshape.9.order_ref
  74.2 25.4 %all-to-all-done.src_ref = s16[4,4,8,32,256]{4,3,2,1,0:T(8,128)(2,1)S(1)} async-done(((s16[4,4,8,32,256]{4,3,2,1,0:T(8,128)(2,1)}), s16[4,4,8,32,256]{4,3,2,1,0:T(8,128)(2,1)S(1)}, u32[]{:S(2)}, u32[]{:S(2)}) %all-to-all-start) | async-done | bytes 2097184 | tf_op jit(solution)/shard_map/all_to_all | solution.py:279
  99.6 0.0 copy-start
  99.6 1.4 copy-done
  100.9 6.2 %merge.1 = s16[8,4,32,256]{3,2,1,0:T(8,128)(2,1)} custom-call(s32[32]{0:T(128)} %reshape.9.order_ref, s16[4,4,8,32,256]{4,3,2,1,0:T(8,128)(2,1)} %copy-done), custom_call_target="tpu_custom_call" | custom-call | tf_op jit(solution)/shard_map/merge/pallas_call | solution.py:240
  107.1 24.0 %all_to_all.10.src_ref = s16[8,4,32,256]{3,2,1,0:T(8,128)(2,1)} all-to-all(s16[8,4,32,256]{3,2,1,0:T(8,128)(2,1)} %merge.1), channel_id=1, replica_groups=mesh['bx'=8,'bz'=4] {'bx'}, dimensions={0} | all-to-all | bytes 1048576 | tf_op jit(solution)/shard_map/all_to_all | solution.py:281
  131.1 4.9 %open_image.1 = f32[4,32,2048]{2,1,0:T(8,128)} custom-call(s16[8,4,32,256]{3,2,1,0:T(8,128)(2,1)} %all_to_all.10.src_ref), custom_call_target="tpu_custom_call" | custom-call | tf_op jit(solution)/shard_map/open_image/pallas_call | solution.py:259
Async XLA Ops:
  0.0 12.8 %copy-start.2 = (f32[8,3]{0,1:T(4,128)S(1)}, f32[8,3]{0,1:T(4,128)}, u32[]{:S(2)}) copy-start(f32[8,3]{0,1:T(4,128)} %param.8) | copy-start | bytes 292
  7.8 27.6 %collective-permute-start = (bf16[4,1024,128]{2,1,0:T(8,128)(2,1)}, bf16[4,1024,128]{2,1,0:T(8,128)(2,1)S(1)}, u32[]{:S(2)}, u32[]{:S(2)}) collective-permute-start(bf16[4,1024,128]{2,1,0:T(8,128)(2,1)} %pack_halo.1), channel_id=1, source_target_pairs={{0,4},{4,8},{8,12},{12,16},{16,20},{20,24},{24,28},{1,5},{5,9},{9,... | collective-permute-start | bytes 3145736 | tf_op jit(solution)/shard_map/ppermute | solution.py:276
  35.4 1.0 copy-start.1
  66.0 7.5 %copy-start.3 = (s32[8,4]{0,1:T(4,128)S(1)}, s32[8,4]{0,1:T(4,128)}, u32[]{:S(2)}) copy-start(s32[8,4]{0,1:T(4,128)} %param.10) | copy-start | bytes 388
  66.0 33.6 %all-to-all-start = ((s16[4,4,8,32,256]{4,3,2,1,0:T(8,128)(2,1)}), s16[4,4,8,32,256]{4,3,2,1,0:T(8,128)(2,1)S(1)}, u32[]{:S(2)}, u32[]{:S(2)}) async-start(s16[4,4,8,32,256]{4,3,2,1,0:T(8,128)(2,1)} %volume.1), calls=%async_computation | async-start | bytes 4194304 | tf_op jit(solution)/shard_map/all_to_all | solution.py:279
  99.6 1.4 copy-start

commit v3 on v2

--- a/solution.py
+++ b/solution.py
@@ -1,4 +1,5 @@
 import functools
+import math
 
 import jax
 import jax.numpy as jnp
@@ -7,10 +8,12 @@
 from jax.experimental.pallas import tpu as pltpu
 from jax.sharding import PartitionSpec as P
 
+
 LANES = 128
 SUB = 16
 LOG2E = 1.4426950408889634
 CODE = 65535.0
+CHUNKS = 2
 
 
 def encode(value):
@@ -48,16 +51,24 @@
             dst_ref[f, :, v * LANES : (v + 1) * LANES] = total.astype(jnp.bfloat16)
 
 
-def pack_halo(fields, pitch):
+def pack_halo(fields, pitch, chunk, chunks):
     nf, slices, height, width = fields.shape
-    rows = 128
+    rows = 64
     lanes = -(-slices * pitch // LANES) * LANES
+    steps = height // chunks // rows
     return pl.pallas_call(
         functools.partial(pack_kernel, pitch),
-        grid=(height // rows,),
-        in_specs=[pl.BlockSpec((nf, slices, rows, LANES), lambda r: (0, 0, r, width // LANES - 1))],
+        grid=(steps,),
+        in_specs=[
+            pl.BlockSpec((nf, slices, rows, LANES), lambda r: (0, 0, r + chunk * steps, width // LANES - 1))
+        ],
         out_specs=pl.BlockSpec((nf, rows, lanes), lambda r: (0, r, 0)),
-        out_shape=jax.ShapeDtypeStruct((nf, height, lanes), jnp.bfloat16),
+        out_shape=jax.ShapeDtypeStruct((nf, height // chunks, lanes), jnp.bfloat16),
+        cost_estimate=pl.CostEstimate(
+            flops=height // chunks * LANES * nf * slices * 4,
+            bytes_accessed=height // chunks * LANES * nf * slices * 2,
+            transcendentals=0,
+        ),
         name="pack_halo",
     )(fields)
 
@@ -118,7 +129,8 @@
     return [jnp.where(lane == LANES - 1, rolled[(i + 1) % n], rolled[i]) for i in range(n)]
 
 
-def volume_kernel(pitch, marks_ref, color_ref, opacity_ref, live_ref, fields_ref, halo_ref, out_ref, tab_ref):
+def volume_kernel(pitch, first_step, marks_ref, color_ref, opacity_ref, live_ref, fields_ref, halo_ref, *rest):
+    out_ref, tab_ref = rest[-2:]
     nf, slices, rows, width = fields_ref.shape
     nv = width // LANES
     per = LANES // pitch
@@ -130,7 +142,7 @@
 
     low = live_ref[0]
     high = live_ref[1]
-    row0 = step * rows
+    row0 = (step + first_step) * rows
     alive = (row0 < high) & (row0 + rows > low)
     edge = jnp.where(lax.axis_index("bx") > 0, 1.0, 0.0).astype(jnp.float32)
     base = 3 * (lax.axis_index("bz") * slices) // 8
@@ -193,27 +205,32 @@
         lax.fori_loop(0, rows // SUB, group, 0)
 
 
-def volume(fields, halo, breakpoints, tf_color, tf_opacity, live, pitch, count_x, count_z):
+def volume(fields, halo, packed, breakpoints, tf_color, tf_opacity, live, pitch, count_x, count_z, chunk, chunks):
     nf, slices, height, width = fields.shape
     assert slices % 8 == 0
     owned = height // (count_x * count_z)
+    part_x = count_x // chunks
+    steps = part_x * count_z
+    cells = slices * height // chunks * width
     smem = pl.BlockSpec(memory_space=pltpu.SMEM)
     return pl.pallas_call(
-        functools.partial(volume_kernel, pitch),
-        grid=(count_x * count_z,),
+        functools.partial(volume_kernel, pitch, chunk * steps),
+        grid=(steps,),
         in_specs=[
             smem,
             smem,
             smem,
             smem,
-            pl.BlockSpec((nf, slices, owned, width), lambda r: (0, 0, r, 0)),
+            pl.BlockSpec((nf, slices, owned, width), lambda r: (0, 0, r + chunk * steps, 0)),
             pl.BlockSpec((nf, owned, halo.shape[2]), lambda r: (0, r, 0)),
+            *[pl.BlockSpec(memory_space=pl.ANY) for _ in packed],
         ],
         out_specs=pl.BlockSpec((1, 4, 1, owned, width), lambda r: (r % count_z, 0, r // count_z, 0, 0)),
-        out_shape=jax.ShapeDtypeStruct((count_z, 4, count_x, owned, width), jnp.int16),
+        out_shape=jax.ShapeDtypeStruct((count_z, 4, part_x, owned, width), jnp.int16),
         scratch_shapes=[pltpu.VMEM((8, 8, LANES), jnp.float32)],
+        cost_estimate=pl.CostEstimate(flops=cells * 100, bytes_accessed=cells * 40, transcendentals=cells * 2),
         name="volume",
-    )(breakpoints, tf_color.reshape(-1), tf_opacity, live, fields, halo)
+    )(breakpoints, tf_color, tf_opacity, live, fields, halo, *packed)
 
 
 def merge_kernel(order_ref, src_ref, dst_ref):
@@ -272,12 +289,22 @@
     count_z = lax.axis_size("bz")
     reach = 3 * (slices * count_z - 1) // 8 + 1
     pitch = halo_pitch(reach)
-    rim = pack_halo(fields, pitch)
-    halo = lax.ppermute(rim, "bx", [(i, i + 1) for i in range(count_x - 1)])
+    chunks = math.gcd(CHUNKS, count_x)
     live = live_rows.reshape(2)
-    partial = volume(fields, halo, breakpoints, tf_color, tf_opacity, live, pitch, count_x, count_z)
-    arrived = lax.all_to_all(partial, "bz", split_axis=0, concat_axis=0, tiled=True)
-    merged = merge(arrived, depth_order)
+    colors = tf_color.reshape(-1)
+    route = [(i, i + 1) for i in range(count_x - 1)]
+    rims = [pack_halo(fields, pitch, c, chunks) for c in range(chunks)]
+    halos = []
+    for c in range(chunks):
+        halos.append(lax.ppermute(rims[c], "bx", route))
+    merged = []
+    for c in range(chunks):
+        partial = volume(
+            fields, halos[c], rims, breakpoints, colors, tf_opacity, live, pitch, count_x, count_z, c, chunks
+        )
+        arrived = lax.all_to_all(partial, "bz", split_axis=0, concat_axis=0, tiled=True)
+        merged.append(merge(arrived, depth_order))
+    merged = jnp.concatenate(merged, axis=0)
     moved = lax.all_to_all(merged, "bx", split_axis=0, concat_axis=0, tiled=True)
     return open_image(moved)
 

time: 138 us -> 136 us (0.986)
  waiting for transfers between devices: 47.3 us -> 26.6 us
  Pallas kernels: 48.5 us -> 61.6 us
  starting transfers between devices: 12.4 us -> 16.8 us
    all_to_all x1 -> x2, waiting for transfers between devices: 25.4 us -> 10 us  [per_device(): lax.all_to_all(partial, 'bz', split_axis=0, concat_axis=0, tiled=True)]
    pallas_call x2 -> x4, Pallas kernels: 37.4 us -> 49.3 us  [the longest x2 36.5 us: volume(): pl.pallas_call(functools.partial(volume_kernel, pitch, chunk * steps), gr...]
    ppermute x1 -> x2, waiting for transfers between devices: 21.9 us -> 16.6 us  [per_device(): halos.append(lax.ppermute(rims[c], 'bx', route))]
    ppermute x1 -> x2, starting transfers between devices: 4.92 us -> 9.75 us  [per_device(): halos.append(lax.ppermute(rims[c], 'bx', route))]
    pallas_call x1 -> x2, Pallas kernels: 6.17 us -> 7.32 us  [merge(): pl.pallas_call(merge_kernel, grid=(count_x,), in_specs=[pl.BlockSpec(memo...]
    all_to_all x1 -> x2, starting transfers between devices: 7.45 us -> 7.04 us  [per_device(): lax.all_to_all(partial, 'bz', split_axis=0, concat_axis=0, tiled=True)]
  transfers between devices with their start and end apart: 2 -> 4, of which waited for: 2 -> 3; matrix products, arithmetic and copies ran while one was open for 1% -> 1% of each run, Pallas kernels for 0% -> 22%
where the time goes in v3:
time: 136 us; the launch traced here: 134 us
  Pallas kernels  61.6 us (45%)
  waiting for transfers between devices  26.6 us (20%)
  blocking collectives  24.1 us (18%)
  starting transfers between devices  16.8 us (12%)
  local copies, waits for them, and re-layouts  3.96 us (3%)
    pallas_call x2, Pallas kernels, volume(): pl.pallas_call(functools.partial(volume_kernel, pitch, chunk * steps), gr...  36.5 us
    all_to_all x1, blocking collectives, per_device(): lax.all_to_all(merged, 'bx', split_axis=0, concat_axis=0, tiled=True)  24.1 us
    ppermute x2, waiting for transfers between devices, per_device(): halos.append(lax.ppermute(rims[c], 'bx', route))  16.6 us
    pallas_call x2, Pallas kernels, pack_halo(): pl.pallas_call(functools.partial(pack_kernel, pitch), grid=(steps,), in_s...  12.8 us
    all_to_all x2, waiting for transfers between devices, per_device(): lax.all_to_all(partial, 'bz', split_axis=0, concat_axis=0, tiled=True)  10 us
    ppermute x2, starting transfers between devices, per_device(): halos.append(lax.ppermute(rims[c], 'bx', route))  9.75 us
    pallas_call x2, Pallas kernels, merge(): pl.pallas_call(merge_kernel, grid=(count_x,), in_specs=[pl.BlockSpec(memo...  7.32 us
    all_to_all x2, starting transfers between devices, per_device(): lax.all_to_all(partial, 'bz', split_axis=0, concat_axis=0, tiled=True)  7.04 us
  transfers between devices with their start and end apart: 4, of which 3 were waited for; matrix products, arithmetic and copies ran while one was open for 1% of the time, Pallas kernels for 22%

profile of v3, /device:TPU:0, one launch (start us, length us, event | category | flops | bytes accessed | tf_op | source)
XLA Modules:
  0.0 134.2 jit_solution(18385257815361290129)
XLA Ops:
  0.0 6.4 %pack_halo.2.rest_0_ = bf16[4,512,128]{2,1,0:T(8,128)(2,1)} custom-call(bf16[4,8,1024,256]{3,2,1,0:T(8,128)(2,1)} %fields_ref.3), custom_call_target="tpu_custom_call" | custom-call | flops 8388608 | bytes 4194304 | tf_op jit(solution)/shard_map/pack_halo/pallas_call | solution.py:59
  6.4 4.9 %collective-permute-start = (bf16[4,512,128]{2,1,0:T(8,128)(2,1)}, bf16[4,512,128]{2,1,0:T(8,128)(2,1)S(1)}, u32[]{:S(2)}, u32[]{:S(2)}) collective-permute-start(bf16[4,512,128]{2,1,0:T(8,128)(2,1)} %pack_halo.2.rest_0_), channel_id=1, source_target_pairs={{0,4},{4,8},{8,12},{12,16},{16,20},{20,24},{24,28},{1,5},{5,9},{9,... | collective-permute-start | bytes 1572872 | tf_op jit(solution)/shard_map/ppermute | solution.py:299
  11.3 0.1 copy.10
  11.4 0.6 reshape.11.color_ref
  12.0 6.4 %pack_halo.3.rest_1_ = bf16[4,512,128]{2,1,0:T(8,128)(2,1)} custom-call(bf16[4,8,1024,256]{3,2,1,0:T(8,128)(2,1)} %fields_ref.3), custom_call_target="tpu_custom_call" | custom-call | flops 8388608 | bytes 4194304 | tf_op jit(solution)/shard_map/pack_halo/pallas_call | solution.py:59
  18.4 4.4 %collective-permute-done.halo_ref = bf16[4,512,128]{2,1,0:T(8,128)(2,1)S(1)} collective-permute-done((bf16[4,512,128]{2,1,0:T(8,128)(2,1)}, bf16[4,512,128]{2,1,0:T(8,128)(2,1)S(1)}, u32[]{:S(2)}, u32[]{:S(2)}) %collective-permute-start) | collective-permute-done | bytes 524320 | tf_op jit(solution)/shard_map/ppermute | solution.py:299
  22.8 0.8 copy-done.3
  23.5 17.6 %volume.2 = s16[4,4,4,32,256]{4,3,2,1,0:T(8,128)(2,1)} custom-call(s32[8]{0:T(128)} %marks_ref.3, f32[24]{0:T(128)} %reshape.11.color_ref, f32[8]{0:T(128)} %opacity_ref.3, s32[2]{0:T(128)} %bitcast.1, bf16[4,8,1024,256]{3,2,1,0:T(8,128)(2,1)} %fields_ref.3, bf16[4,512,128]{2,1,0:T(8,128)(2,1)} %copy-done.3, bf16[4,512,128]{2,1,0:T(8,128)(2,1)} %pack_halo.2.rest_0_, ...), custom_call_target="tpu_custom_call" | custom-call | flops 104857600 | bytes 41943040 | tf_op jit(solution)/shard_map/volume/pallas_call | solution.py:216
  41.1 3.5 %all-to-all-start = ((s16[4,4,4,32,256]{4,3,2,1,0:T(8,128)(2,1)}), s16[4,4,4,32,256]{4,3,2,1,0:T(8,128)(2,1)S(1)}, u32[]{:S(2)}, u32[]{:S(2)}) async-start(s16[4,4,4,32,256]{4,3,2,1,0:T(8,128)(2,1)} %volume.2), calls=%async_computation | async-start | bytes 2097152 | tf_op jit(solution)/shard_map/all_to_all | solution.py:305
  44.7 4.9 %collective-permute-start.1 = (bf16[4,512,128]{2,1,0:T(8,128)(2,1)S(1)}, bf16[4,512,128]{2,1,0:T(8,128)(2,1)S(1)}, u32[]{:S(2)}, u32[]{:S(2)}) collective-permute-start(bf16[4,512,128]{2,1,0:T(8,128)(2,1)S(1)} %copy-done), channel_id=1, source_target_pairs={{0,4},{4,8},{8,12},{12,16},{16,20},{20,24},{24,28},{1,5},{5,9},{9,... | collective-permute-start | bytes 1572872 | tf_op jit(solution)/shard_map/ppermute | solution.py:299
  49.5 12.2 %collective-permute-done.1.halo_ref = bf16[4,512,128]{2,1,0:T(8,128)(2,1)S(1)} collective-permute-done((bf16[4,512,128]{2,1,0:T(8,128)(2,1)S(1)}, bf16[4,512,128]{2,1,0:T(8,128)(2,1)S(1)}, u32[]{:S(2)}, u32[]{:S(2)}) %collective-permute-start.1) | collective-permute-done | bytes 524320 | tf_op jit(solution)/shard_map/ppermute | solution.py:299
  61.8 0.8 copy-done.4
  62.6 19.0 %volume.3 = s16[4,4,4,32,256]{4,3,2,1,0:T(8,128)(2,1)} custom-call(s32[8]{0:T(128)} %marks_ref.3, f32[24]{0:T(128)} %reshape.11.color_ref, f32[8]{0:T(128)} %opacity_ref.3, s32[2]{0:T(128)} %bitcast.2, bf16[4,8,1024,256]{3,2,1,0:T(8,128)(2,1)} %fields_ref.3, bf16[4,512,128]{2,1,0:T(8,128)(2,1)} %copy-done.4, bf16[4,512,128]{2,1,0:T(8,128)(2,1)} %pack_halo.2.rest_0_, ...), custom_call_target="tpu_custom_call" | custom-call | flops 104857600 | bytes 41943040 | tf_op jit(solution)/shard_map/volume/pallas_call | solution.py:216
  81.5 0.0 all-to-all-done.src_ref
  81.5 3.5 %all-to-all-start.1 = ((s16[4,4,4,32,256]{4,3,2,1,0:T(8,128)(2,1)}), s16[4,4,4,32,256]{4,3,2,1,0:T(8,128)(2,1)S(1)}, u32[]{:S(2)}, u32[]{:S(2)}) async-start(s16[4,4,4,32,256]{4,3,2,1,0:T(8,128)(2,1)} %volume.3), calls=%async_computation.1 | async-start | bytes 2097152 | tf_op jit(solution)/shard_map/all_to_all | solution.py:305
  85.1 0.1 copy.9
  85.2 0.6 reshape.10.order_ref
  85.8 3.7 %merge.2 = s16[4,4,32,256]{3,2,1,0:T(8,128)(2,1)} custom-call(s32[32]{0:T(128)} %reshape.10.order_ref, s16[4,4,4,32,256]{4,3,2,1,0:T(8,128)(2,1)} %copy-done.1), custom_call_target="tpu_custom_call" | custom-call | tf_op jit(solution)/shard_map/merge/pallas_call | solution.py:257
  89.4 10.0 %all-to-all-done.1.src_ref = s16[4,4,4,32,256]{4,3,2,1,0:T(8,128)(2,1)S(1)} async-done(((s16[4,4,4,32,256]{4,3,2,1,0:T(8,128)(2,1)}), s16[4,4,4,32,256]{4,3,2,1,0:T(8,128)(2,1)S(1)}, u32[]{:S(2)}, u32[]{:S(2)}) %all-to-all-start.1) | async-done | bytes 1048608 | tf_op jit(solution)/shard_map/all_to_all | solution.py:305
  99.5 1.0 copy-done.2
  100.4 3.7 %merge.3 = s16[4,4,32,256]{3,2,1,0:T(8,128)(2,1)} custom-call(s32[32]{0:T(128)} %reshape.10.order_ref, s16[4,4,4,32,256]{4,3,2,1,0:T(8,128)(2,1)} %copy-done.2), custom_call_target="tpu_custom_call" | custom-call | tf_op jit(solution)/shard_map/merge/pallas_call | solution.py:257
  104.1 1.1 pad_add_fusion
  105.2 24.1 %all_to_all.15.src_ref = s16[8,4,32,256]{3,2,1,0:T(8,128)(2,1)} all-to-all(s16[8,4,32,256]{3,2,1,0:T(8,128)(2,1)S(1)} %pad_add_fusion), channel_id=1, replica_groups=mesh['bx'=8,'bz'=4] {'bx'}, dimensions={0} | all-to-all | bytes 1048576 | tf_op jit(solution)/shard_map/all_to_all | solution.py:308
  129.3 4.9 %open_image.1 = f32[4,32,2048]{2,1,0:T(8,128)} custom-call(s16[8,4,32,256]{3,2,1,0:T(8,128)(2,1)} %all_to_all.15.src_ref), custom_call_target="tpu_custom_call" | custom-call | tf_op jit(solution)/shard_map/open_image/pallas_call | solution.py:276
  (11 shorter events, 0.0 us)
Async XLA Ops:
  0.0 11.3 %copy-start.5 = (f32[8,3]{0,1:T(4,128)S(1)}, f32[8,3]{0,1:T(4,128)}, u32[]{:S(2)}) copy-start(f32[8,3]{0,1:T(4,128)} %param.8) | copy-start | bytes 292
  6.4 16.3 %collective-permute-start = (bf16[4,512,128]{2,1,0:T(8,128)(2,1)}, bf16[4,512,128]{2,1,0:T(8,128)(2,1)S(1)}, u32[]{:S(2)}, u32[]{:S(2)}) collective-permute-start(bf16[4,512,128]{2,1,0:T(8,128)(2,1)} %pack_halo.2.rest_0_), channel_id=1, source_target_pairs={{0,4},{4,8},{8,12},{12,16},{16,20},{20,24},{24,28},{1,5},{5,9},{9,... | collective-permute-start | bytes 1572872 | tf_op jit(solution)/shard_map/ppermute | solution.py:299
  18.4 26.3 %copy-start = (bf16[4,512,128]{2,1,0:T(8,128)(2,1)S(1)}, bf16[4,512,128]{2,1,0:T(8,128)(2,1)}, u32[]{:S(2)}) copy-start(bf16[4,512,128]{2,1,0:T(8,128)(2,1)} %pack_halo.3.rest_1_) | copy-start | bytes 1572868
  22.8 0.8 copy-start.3
  23.5 61.5 %copy-start.6 = (s32[8,4]{0,1:T(4,128)S(1)}, s32[8,4]{0,1:T(4,128)}, u32[]{:S(2)}) copy-start(s32[8,4]{0,1:T(4,128)} %param.10) | copy-start | bytes 388
  41.1 40.4 %all-to-all-start = ((s16[4,4,4,32,256]{4,3,2,1,0:T(8,128)(2,1)}), s16[4,4,4,32,256]{4,3,2,1,0:T(8,128)(2,1)S(1)}, u32[]{:S(2)}, u32[]{:S(2)}) async-start(s16[4,4,4,32,256]{4,3,2,1,0:T(8,128)(2,1)} %volume.2), calls=%async_computation | async-start | bytes 2097152 | tf_op jit(solution)/shard_map/all_to_all | solution.py:305
  44.7 17.1 %collective-permute-start.1 = (bf16[4,512,128]{2,1,0:T(8,128)(2,1)S(1)}, bf16[4,512,128]{2,1,0:T(8,128)(2,1)S(1)}, u32[]{:S(2)}, u32[]{:S(2)}) collective-permute-start(bf16[4,512,128]{2,1,0:T(8,128)(2,1)S(1)} %copy-done), channel_id=1, source_target_pairs={{0,4},{4,8},{8,12},{12,16},{16,20},{20,24},{24,28},{1,5},{5,9},{9,... | collective-permute-start | bytes 1572872 | tf_op jit(solution)/shard_map/ppermute | solution.py:299
  61.8 0.8 copy-start.4
  81.5 4.3 %copy-start.1 = (s16[4,4,4,32,256]{4,3,2,1,0:T(8,128)(2,1)}, s16[4,4,4,32,256]{4,3,2,1,0:T(8,128)(2,1)S(1)}, u32[]{:S(2)}) copy-start(s16[4,4,4,32,256]{4,3,2,1,0:T(8,128)(2,1)S(1)} %all-to-all-done.src_ref) | copy-start | bytes 3145732
  81.5 17.9 %all-to-all-start.1 = ((s16[4,4,4,32,256]{4,3,2,1,0:T(8,128)(2,1)}), s16[4,4,4,32,256]{4,3,2,1,0:T(8,128)(2,1)S(1)}, u32[]{:S(2)}, u32[]{:S(2)}) async-start(s16[4,4,4,32,256]{4,3,2,1,0:T(8,128)(2,1)} %volume.3), calls=%async_computation.1 | async-start | bytes 2097152 | tf_op jit(solution)/shard_map/all_to_all | solution.py:305
  99.5 1.0 copy-start.2

commit v4 on v3

--- a/solution.py
+++ b/solution.py
@@ -53,7 +53,7 @@
 
 def pack_halo(fields, pitch, chunk, chunks):
     nf, slices, height, width = fields.shape
-    rows = 64
+    rows = math.gcd(256, height // chunks)
     lanes = -(-slices * pitch // LANES) * LANES
     steps = height // chunks // rows
     return pl.pallas_call(
@@ -237,47 +237,52 @@
     depth = src_ref.shape[0]
     column = lax.axis_index("bx")
     rows = src_ref.shape[3]
-    for g in range(0, rows, SUB):
-        at = slice(g, g + SUB)
-        total = None
-        for k in range(depth):
-            d = order_ref[column * depth + k]
-            part = [decode(src_ref[d, q, 0, at]) for q in range(4)]
-            if total is None:
-                total = part
-            else:
-                clear = 1.0 - total[3]
-                total = [t + clear * p for t, p in zip(total, part)]
-        for q in range(4):
-            dst_ref[0, q, at] = encode(total[q])
+    for i in range(dst_ref.shape[0]):
+        for g in range(0, rows, SUB):
+            at = slice(g, g + SUB)
+            total = None
+            for k in range(depth):
+                d = order_ref[column * depth + k]
+                part = [decode(src_ref[d, q, i, at]) for q in range(4)]
+                if total is None:
+                    total = part
+                else:
+                    clear = 1.0 - total[3]
+                    total = [t + clear * p for t, p in zip(total, part)]
+            for q in range(4):
+                dst_ref[i, q, at] = encode(total[q])
 
 
 def merge(arrived, order):
     depth, _, count_x, owned, width = arrived.shape
+    many = math.gcd(2, count_x)
     return pl.pallas_call(
         merge_kernel,
-        grid=(count_x,),
+        grid=(count_x // many,),
         in_specs=[
             pl.BlockSpec(memory_space=pltpu.SMEM),
-            pl.BlockSpec((depth, 4, 1, owned, width), lambda i: (0, 0, i, 0, 0)),
+            pl.BlockSpec((depth, 4, many, owned, width), lambda i: (0, 0, i, 0, 0)),
         ],
-        out_specs=pl.BlockSpec((1, 4, owned, width), lambda i: (i, 0, 0, 0)),
+        out_specs=pl.BlockSpec((many, 4, owned, width), lambda i: (i, 0, 0, 0)),
         out_shape=jax.ShapeDtypeStruct((count_x, 4, owned, width), jnp.int16),
         name="merge",
     )(order.reshape(-1), arrived)
 
 
 def open_kernel(src_ref, dst_ref):
-    dst_ref[...] = decode(src_ref[0])
+    width = src_ref.shape[3]
+    for i in range(src_ref.shape[0]):
+        dst_ref[:, :, i * width : (i + 1) * width] = decode(src_ref[i])
 
 
 def open_image(moved):
     count_x, _, owned, width = moved.shape
+    many = math.gcd(4, count_x)
     return pl.pallas_call(
         open_kernel,
-        grid=(count_x,),
-        in_specs=[pl.BlockSpec((1, 4, owned, width), lambda i: (i, 0, 0, 0))],
-        out_specs=pl.BlockSpec((4, owned, width), lambda i: (0, 0, i)),
+        grid=(count_x // many,),
+        in_specs=[pl.BlockSpec((many, 4, owned, width), lambda i: (i, 0, 0, 0))],
+        out_specs=pl.BlockSpec((4, owned, many * width), lambda i: (0, 0, i)),
         out_shape=jax.ShapeDtypeStruct((4, owned, count_x * width), jnp.float32),
         name="open_image",
     )(moved)

time: 136 us -> 128 us (0.941)
  Pallas kernels: 61.6 us -> 50.8 us
  waiting for transfers between devices: 26.6 us -> 30.5 us
    pallas_call x2, Pallas kernels: 12.8 us -> 7.01 us  [pack_halo(): pl.pallas_call(functools.partial(pack_kernel, pitch), grid=(steps,), in_s...]
    pallas_call x3, Pallas kernels: 12.3 us -> 7.25 us  [the longest x2 5.23 us: merge(): pl.pallas_call(merge_kernel, grid=(count_x // many,), in_specs=[pl.BlockS...]
    ppermute x2, waiting for transfers between devices: 16.6 us -> 19.5 us  [per_device(): halos.append(lax.ppermute(rims[c], 'bx', route))]
  transfers between devices with their start and end apart: 4 -> 4, of which waited for: 3 -> 3; matrix products, arithmetic and copies ran while one was open for 1% -> 1% of each run, Pallas kernels for 22% -> 20%
where the time goes in v4:
time: 128 us; the launch traced here: 127 us
  Pallas kernels  50.8 us (40%)
  waiting for transfers between devices  30.5 us (24%)
  blocking collectives  24.1 us (19%)
  starting transfers between devices  16.8 us (13%)
  local copies, waits for them, and re-layouts  3.96 us (3%)
    pallas_call x2, Pallas kernels, volume(): pl.pallas_call(functools.partial(volume_kernel, pitch, chunk * steps), gr...  36.5 us
    all_to_all x1, blocking collectives, per_device(): lax.all_to_all(merged, 'bx', split_axis=0, concat_axis=0, tiled=True)  24.1 us
    ppermute x2, waiting for transfers between devices, per_device(): halos.append(lax.ppermute(rims[c], 'bx', route))  19.5 us
    all_to_all x2, waiting for transfers between devices, per_device(): lax.all_to_all(partial, 'bz', split_axis=0, concat_axis=0, tiled=True)  11.1 us
    ppermute x2, starting transfers between devices, per_device(): halos.append(lax.ppermute(rims[c], 'bx', route))  9.75 us
    all_to_all x2, starting transfers between devices, per_device(): lax.all_to_all(partial, 'bz', split_axis=0, concat_axis=0, tiled=True)  7.04 us
    pallas_call x2, Pallas kernels, pack_halo(): pl.pallas_call(functools.partial(pack_kernel, pitch), grid=(steps,), in_s...  7.01 us
    pallas_call x2, Pallas kernels, merge(): pl.pallas_call(merge_kernel, grid=(count_x // many,), in_specs=[pl.BlockS...  5.23 us
  transfers between devices with their start and end apart: 4, of which 3 were waited for; matrix products, arithmetic and copies ran while one was open for 1% of the time, Pallas kernels for 20%

profile of v4, /device:TPU:0, one launch (start us, length us, event | category | flops | bytes accessed | tf_op | source)
XLA Modules:
  0.0 127.3 jit_solution(12909040666210048486)
XLA Ops:
  0.0 3.5 %pack_halo.2.rest_0_ = bf16[4,512,128]{2,1,0:T(8,128)(2,1)} custom-call(bf16[4,8,1024,256]{3,2,1,0:T(8,128)(2,1)} %fields_ref.3), custom_call_target="tpu_custom_call" | custom-call | flops 8388608 | bytes 4194304 | tf_op jit(solution)/shard_map/pack_halo/pallas_call | solution.py:59
  3.5 4.9 %collective-permute-start = (bf16[4,512,128]{2,1,0:T(8,128)(2,1)}, bf16[4,512,128]{2,1,0:T(8,128)(2,1)S(1)}, u32[]{:S(2)}, u32[]{:S(2)}) collective-permute-start(bf16[4,512,128]{2,1,0:T(8,128)(2,1)} %pack_halo.2.rest_0_), channel_id=1, source_target_pairs={{0,4},{4,8},{8,12},{12,16},{16,20},{20,24},{24,28},{1,5},{5,9},{9,... | collective-permute-start | bytes 1572872 | tf_op jit(solution)/shard_map/ppermute | solution.py:304
  8.4 0.1 copy.10
  8.5 0.6 reshape.11.color_ref
  9.1 3.5 %pack_halo.3.rest_1_ = bf16[4,512,128]{2,1,0:T(8,128)(2,1)} custom-call(bf16[4,8,1024,256]{3,2,1,0:T(8,128)(2,1)} %fields_ref.3), custom_call_target="tpu_custom_call" | custom-call | flops 8388608 | bytes 4194304 | tf_op jit(solution)/shard_map/pack_halo/pallas_call | solution.py:59
  12.6 7.3 %collective-permute-done.halo_ref = bf16[4,512,128]{2,1,0:T(8,128)(2,1)S(1)} collective-permute-done((bf16[4,512,128]{2,1,0:T(8,128)(2,1)}, bf16[4,512,128]{2,1,0:T(8,128)(2,1)S(1)}, u32[]{:S(2)}, u32[]{:S(2)}) %collective-permute-start) | collective-permute-done | bytes 524320 | tf_op jit(solution)/shard_map/ppermute | solution.py:304
  19.9 0.8 copy-done.3
  20.7 17.6 %volume.2 = s16[4,4,4,32,256]{4,3,2,1,0:T(8,128)(2,1)} custom-call(s32[8]{0:T(128)} %marks_ref.3, f32[24]{0:T(128)} %reshape.11.color_ref, f32[8]{0:T(128)} %opacity_ref.3, s32[2]{0:T(128)} %bitcast.1, bf16[4,8,1024,256]{3,2,1,0:T(8,128)(2,1)} %fields_ref.3, bf16[4,512,128]{2,1,0:T(8,128)(2,1)} %copy-done.3, bf16[4,512,128]{2,1,0:T(8,128)(2,1)} %pack_halo.2.rest_0_, ...), custom_call_target="tpu_custom_call" | custom-call | flops 104857600 | bytes 41943040 | tf_op jit(solution)/shard_map/volume/pallas_call | solution.py:216
  38.2 3.5 %all-to-all-start = ((s16[4,4,4,32,256]{4,3,2,1,0:T(8,128)(2,1)}), s16[4,4,4,32,256]{4,3,2,1,0:T(8,128)(2,1)S(1)}, u32[]{:S(2)}, u32[]{:S(2)}) async-start(s16[4,4,4,32,256]{4,3,2,1,0:T(8,128)(2,1)} %volume.2), calls=%async_computation | async-start | bytes 2097152 | tf_op jit(solution)/shard_map/all_to_all | solution.py:310
  41.8 4.9 %collective-permute-start.1 = (bf16[4,512,128]{2,1,0:T(8,128)(2,1)S(1)}, bf16[4,512,128]{2,1,0:T(8,128)(2,1)S(1)}, u32[]{:S(2)}, u32[]{:S(2)}) collective-permute-start(bf16[4,512,128]{2,1,0:T(8,128)(2,1)S(1)} %copy-done), channel_id=1, source_target_pairs={{0,4},{4,8},{8,12},{12,16},{16,20},{20,24},{24,28},{1,5},{5,9},{9,... | collective-permute-start | bytes 1572872 | tf_op jit(solution)/shard_map/ppermute | solution.py:304
  46.6 12.2 %collective-permute-done.1.halo_ref = bf16[4,512,128]{2,1,0:T(8,128)(2,1)S(1)} collective-permute-done((bf16[4,512,128]{2,1,0:T(8,128)(2,1)S(1)}, bf16[4,512,128]{2,1,0:T(8,128)(2,1)S(1)}, u32[]{:S(2)}, u32[]{:S(2)}) %collective-permute-start.1) | collective-permute-done | bytes 524320 | tf_op jit(solution)/shard_map/ppermute | solution.py:304
  58.9 0.8 copy-done.4
  59.7 19.0 %volume.3 = s16[4,4,4,32,256]{4,3,2,1,0:T(8,128)(2,1)} custom-call(s32[8]{0:T(128)} %marks_ref.3, f32[24]{0:T(128)} %reshape.11.color_ref, f32[8]{0:T(128)} %opacity_ref.3, s32[2]{0:T(128)} %bitcast.2, bf16[4,8,1024,256]{3,2,1,0:T(8,128)(2,1)} %fields_ref.3, bf16[4,512,128]{2,1,0:T(8,128)(2,1)} %copy-done.4, bf16[4,512,128]{2,1,0:T(8,128)(2,1)} %pack_halo.2.rest_0_, ...), custom_call_target="tpu_custom_call" | custom-call | flops 104857600 | bytes 41943040 | tf_op jit(solution)/shard_map/volume/pallas_call | solution.py:216
  78.6 0.0 all-to-all-done.src_ref
  78.6 3.5 %all-to-all-start.1 = ((s16[4,4,4,32,256]{4,3,2,1,0:T(8,128)(2,1)}), s16[4,4,4,32,256]{4,3,2,1,0:T(8,128)(2,1)S(1)}, u32[]{:S(2)}, u32[]{:S(2)}) async-start(s16[4,4,4,32,256]{4,3,2,1,0:T(8,128)(2,1)} %volume.3), calls=%async_computation.1 | async-start | bytes 2097152 | tf_op jit(solution)/shard_map/all_to_all | solution.py:310
  82.2 0.1 copy.9
  82.3 0.6 reshape.10.order_ref
  82.9 2.6 %merge.2 = s16[4,4,32,256]{3,2,1,0:T(8,128)(2,1)} custom-call(s32[32]{0:T(128)} %reshape.10.order_ref, s16[4,4,4,32,256]{4,3,2,1,0:T(8,128)(2,1)} %copy-done.1), custom_call_target="tpu_custom_call" | custom-call | tf_op jit(solution)/shard_map/merge/pallas_call | solution.py:259
  85.5 11.1 %all-to-all-done.1.src_ref = s16[4,4,4,32,256]{4,3,2,1,0:T(8,128)(2,1)S(1)} async-done(((s16[4,4,4,32,256]{4,3,2,1,0:T(8,128)(2,1)}), s16[4,4,4,32,256]{4,3,2,1,0:T(8,128)(2,1)S(1)}, u32[]{:S(2)}, u32[]{:S(2)}) %all-to-all-start.1) | async-done | bytes 1048608 | tf_op jit(solution)/shard_map/all_to_all | solution.py:310
  96.6 1.0 copy-done.2
  97.5 2.6 %merge.3 = s16[4,4,32,256]{3,2,1,0:T(8,128)(2,1)} custom-call(s32[32]{0:T(128)} %reshape.10.order_ref, s16[4,4,4,32,256]{4,3,2,1,0:T(8,128)(2,1)} %copy-done.2), custom_call_target="tpu_custom_call" | custom-call | tf_op jit(solution)/shard_map/merge/pallas_call | solution.py:259
  100.1 1.1 pad_add_fusion
  101.2 24.1 %all_to_all.15.src_ref = s16[8,4,32,256]{3,2,1,0:T(8,128)(2,1)} all-to-all(s16[8,4,32,256]{3,2,1,0:T(8,128)(2,1)S(1)} %pad_add_fusion), channel_id=1, replica_groups=mesh['bx'=8,'bz'=4] {'bx'}, dimensions={0} | all-to-all | bytes 1048576 | tf_op jit(solution)/shard_map/all_to_all | solution.py:313
  125.3 2.0 %open_image.1 = f32[4,32,2048]{2,1,0:T(8,128)} custom-call(s16[8,4,32,256]{3,2,1,0:T(8,128)(2,1)} %all_to_all.15.src_ref), custom_call_target="tpu_custom_call" | custom-call | tf_op jit(solution)/shard_map/open_image/pallas_call | solution.py:281
  (11 shorter events, 0.0 us)
Async XLA Ops:
  0.0 8.4 %copy-start.5 = (f32[8,3]{0,1:T(4,128)S(1)}, f32[8,3]{0,1:T(4,128)}, u32[]{:S(2)}) copy-start(f32[8,3]{0,1:T(4,128)} %param.8) | copy-start | bytes 292
  3.5 16.3 %collective-permute-start = (bf16[4,512,128]{2,1,0:T(8,128)(2,1)}, bf16[4,512,128]{2,1,0:T(8,128)(2,1)S(1)}, u32[]{:S(2)}, u32[]{:S(2)}) collective-permute-start(bf16[4,512,128]{2,1,0:T(8,128)(2,1)} %pack_halo.2.rest_0_), channel_id=1, source_target_pairs={{0,4},{4,8},{8,12},{12,16},{16,20},{20,24},{24,28},{1,5},{5,9},{9,... | collective-permute-start | bytes 1572872 | tf_op jit(solution)/shard_map/ppermute | solution.py:304
  12.6 29.2 %copy-start = (bf16[4,512,128]{2,1,0:T(8,128)(2,1)S(1)}, bf16[4,512,128]{2,1,0:T(8,128)(2,1)}, u32[]{:S(2)}) copy-start(bf16[4,512,128]{2,1,0:T(8,128)(2,1)} %pack_halo.3.rest_1_) | copy-start | bytes 1572868
  19.9 0.8 copy-start.3
  20.6 61.5 %copy-start.6 = (s32[8,4]{0,1:T(4,128)S(1)}, s32[8,4]{0,1:T(4,128)}, u32[]{:S(2)}) copy-start(s32[8,4]{0,1:T(4,128)} %param.10) | copy-start | bytes 388
  38.2 40.4 %all-to-all-start = ((s16[4,4,4,32,256]{4,3,2,1,0:T(8,128)(2,1)}), s16[4,4,4,32,256]{4,3,2,1,0:T(8,128)(2,1)S(1)}, u32[]{:S(2)}, u32[]{:S(2)}) async-start(s16[4,4,4,32,256]{4,3,2,1,0:T(8,128)(2,1)} %volume.2), calls=%async_computation | async-start | bytes 2097152 | tf_op jit(solution)/shard_map/all_to_all | solution.py:310
  41.8 17.1 %collective-permute-start.1 = (bf16[4,512,128]{2,1,0:T(8,128)(2,1)S(1)}, bf16[4,512,128]{2,1,0:T(8,128)(2,1)S(1)}, u32[]{:S(2)}, u32[]{:S(2)}) collective-permute-start(bf16[4,512,128]{2,1,0:T(8,128)(2,1)S(1)} %copy-done), channel_id=1, source_target_pairs={{0,4},{4,8},{8,12},{12,16},{16,20},{20,24},{24,28},{1,5},{5,9},{9,... | collective-permute-start | bytes 1572872 | tf_op jit(solution)/shard_map/ppermute | solution.py:304
  58.9 0.8 copy-start.4
  78.6 4.3 %copy-start.1 = (s16[4,4,4,32,256]{4,3,2,1,0:T(8,128)(2,1)}, s16[4,4,4,32,256]{4,3,2,1,0:T(8,128)(2,1)S(1)}, u32[]{:S(2)}) copy-start(s16[4,4,4,32,256]{4,3,2,1,0:T(8,128)(2,1)S(1)} %all-to-all-done.src_ref) | copy-start | bytes 3145732
  78.6 17.9 %all-to-all-start.1 = ((s16[4,4,4,32,256]{4,3,2,1,0:T(8,128)(2,1)}), s16[4,4,4,32,256]{4,3,2,1,0:T(8,128)(2,1)S(1)}, u32[]{:S(2)}, u32[]{:S(2)}) async-start(s16[4,4,4,32,256]{4,3,2,1,0:T(8,128)(2,1)} %volume.3), calls=%async_computation.1 | async-start | bytes 2097152 | tf_op jit(solution)/shard_map/all_to_all | solution.py:310
  96.6 1.0 copy-start.2
